TPU v7x, 128 devices: a whole 4x4x4 slice. The times are simulated.
128 devices in a mesh: rows: 64 (over y, x, z), feat: 2 (over core).
Axes of the slice: x: 4, y: 4, z: 4, core: 2. Of those that a mesh axis runs over, the one named last changes fastest.
Arguments:
- blocks: bfloat16 [8192, 8, 128, 128], P('rows', 'feat'), may hold values from -0.1875 to 0.1875
- col_index: int32 [8192, 8], P('rows', 'feat'), may hold values from 0 to 8191, as said below
- row_counts: int32 [8192, 2], P('rows', 'feat'), may hold values from 1 to 4, as said below
- labels: int32 [8192, 128], P('rows'), may hold values 0 or 1
- row_weight: float32 [8192, 128], P('rows'), may hold values from 0.3 to 9
- feature_scale: float32 [8192, 128], P('feat'), may hold values from 0.3 to 3
Outputs:
- solution: float32 [8192, 128], P('feat')
- last_resid: float32 [8192, 128], P('rows')
Inputs may be any that keep to these rules, and one draw needn't show every extreme that they name: `col_index`: a block in slot j of a row block names a feature block of half j // 4, that is from (j // 4) * 4096 to (j // 4 + 1) * 4096 - 1. `row_counts`: some row block of every index of rows has 4 stored blocks in each half; slots from the count on are ignored.
All inputs are finite; a program needn't handle non-finite values. No bound on the sum of `labels` on one device may be relied on, other than what follows from the above.
Results may differ from a plain program's by a relative error of at most 0.0063.
Values may be sent and summed in bfloat16 or wider, within the bound.
No kernel may reach another device: no remote copies, remote signals or barrier semaphores. Data moves between devices by JAX's collectives and lax.ppermute only.
A program may use at most 64 MiB of HBM per device.

v0:
```python
import jax
import jax.numpy as jnp
from jax import lax
from jax.sharding import PartitionSpec as P

ITERS = 2


def body(blocks, col_index, row_counts, labels, row_weight, feature_scale):
    block_side = blocks.shape[2]
    feat_local = feature_scale.shape[0]
    local_col = col_index - lax.axis_index("feat") * feat_local
    live = (lax.broadcasted_iota(jnp.int32, col_index.shape, 1) < row_counts).astype(jnp.float32)

    def backward(resid):
        rowed = (row_weight * resid).astype(jnp.bfloat16)
        terms = jnp.einsum("rsij,ri->rsj", blocks, rowed, preferred_element_type=jnp.float32)
        terms = terms * live[:, :, None]
        partial_value = jax.ops.segment_sum(
            terms.reshape(-1, block_side), local_col.reshape(-1), num_segments=feat_local
        )
        local_sq = jnp.sum(resid * resid)
        squares = lax.psum(local_sq, "rows")
        total = lax.psum(partial_value, "rows")
        return (total, squares)

    def feat_norm(step_vec):
        local_sq = jnp.sum(step_vec * step_vec)
        squares = lax.psum(local_sq, "feat")
        return jnp.sqrt(squares + 1e-06)

    resid = row_weight * (2 * labels - 1).astype(jnp.float32)
    total, squares = backward(resid)
    beta_now = jnp.sqrt(squares + 1e-06)
    unit_rows = resid / beta_now
    step_vec = feature_scale * total / beta_now
    alpha_now = feat_norm(step_vec)
    unit_feat = step_vec / alpha_now
    phi_bar = beta_now
    rho_bar = alpha_now
    search = unit_feat
    solution = jnp.zeros_like(unit_feat)
    for turn in range(ITERS):
        scaled = (feature_scale * unit_feat).astype(jnp.bfloat16)
        picked = jnp.take(scaled, local_col, axis=0)
        forward_terms = jnp.einsum(
            "rsij,rsj->rsi", blocks, picked, preferred_element_type=jnp.float32
        )
        forward_partial_value = jnp.sum(forward_terms * live[:, :, None], axis=1)
        resid = row_weight * lax.psum(forward_partial_value, "feat") - alpha_now * unit_rows
        total, squares = backward(resid)
        beta_now = jnp.sqrt(squares + 1e-06)
        unit_rows = resid / beta_now
        step_vec = feature_scale * total / beta_now - beta_now * unit_feat
        alpha_now = feat_norm(step_vec)
        unit_feat = step_vec / alpha_now
        rho_now = jnp.sqrt(rho_bar * rho_bar + beta_now * beta_now)
        cosine = rho_bar / rho_now
        sine_part = beta_now / rho_now
        theta_now = sine_part * alpha_now
        rho_bar = -cosine * alpha_now
        phi_now = cosine * phi_bar
        phi_bar = sine_part * phi_bar
        solution = solution + phi_now / rho_now * search
        search = unit_feat - theta_now / rho_now * search
    return (solution, resid)


def solution(mesh):
    return jax.shard_map(
        body,
        mesh=mesh,
        in_specs=(
            P("rows", "feat", None, None),
            P("rows", "feat"),
            P("rows", "feat"),
            P("rows", None),
            P("rows", None),
            P("feat", None),
        ),
        out_specs=(P("feat", None), P("rows", None)),
        check_vma=False,
    )
```

profile of v0, /device:TPU:0, one launch (start us, length us, event | category | flops | bytes accessed | tf_op | source)
XLA Modules:
  0.0 674.8 jit_solution(14838331523554784863)
XLA Ops:
  7.2 0.0 all-reduce.5.cloned.1.call-start
  7.2 0.7 fusion.12
  8.0 0.7 compare_and_fusion
  8.7 0.1 copy.10
  8.8 0.1 reshape.56
  8.9 1.5 fusion.13
  10.4 8.0 %fusion.10 = f32[128,1,4,128]{3,1,2,0:T(1,128)S(1)} fusion(bf16[128,4,128,128]{3,2,1,0:T(8,128)(2,1)} %param.8, bf16[128,128,1,1]{1,0,2,3:T(8,128)(2,1)S(1)} %get-tuple-element.13), kind=kOutput, calls=%fused_computation.27 | convolution fusion | flops 16777216 | bytes 17072128 | tf_op jit(solution)/shard_map/rsij,ri->rsj/dot_general | solution.py:17
  18.4 0.2 broadcast_multiply_fusion.1
  18.6 0.0 copy-start
  18.6 3.6 scatter_custom_fusion
  22.3 0.0 all-reduce.5.cloned.1.call-update
  22.3 0.0 all-reduce.7.cloned.1.call-start
  22.4 181.5 %psum.64 = f32[]{:T(128)} all-reduce(f32[]{:T(128)} %get-tuple-element.14), channel_id=1, replica_groups=mesh['rows'=64,'feat'=2] {'rows'}, use_global_device_ids=true, to_apply=%region_3.0 | all-reduce | flops 1 | bytes 8 | tf_op jit(solution)/shard_map/psum | solution.py:23
  204.5 0.1 copy.12
  204.7 0.1 reshape.76
  204.8 0.1 copy.11
  204.9 0.0 all-reduce.5.cloned.1.call-done
  204.9 0.0 copy-done
  204.9 4.0 multiply_reduce_fusion.1
  208.9 3.1 psum.65
  212.7 1.8 multiply_convert_fusion.1
  214.6 1.3 gather_fusion
  215.9 0.2 select_bitcast_fusion.1
  216.1 0.0 copy-start.2
  216.1 0.0 copy-start.3
  216.1 12.3 %fusion.6 = f32[128,4,1,128]{3,2,1,0:T(1,128)S(1)} fusion(bf16[128,4,128,128]{3,2,1,0:T(8,128)(2,1)} %param.8, bf16[128,4,128,1]{2,1,0,3:T(4,128)(2,1)S(1)} %select_bitcast_fusion.1), kind=kOutput, calls=%fused_computation.17 | convolution fusion | flops 16777216 | bytes 17170432 | tf_op jit(solution)/shard_map/rsij,rsj->rsi/dot_general | solution.py:46
  228.4 0.9 multiply_reduce_fusion.3
  229.3 0.0 all-reduce.7.cloned.1.call-update
  229.3 0.2 all-reduce.9.cloned.1.call-start
  229.5 16.6 %all-reduce.7.cloned.1.call-done = f32[128,128]{1,0:T(8,128)} async-done(((f32[128,128]{1,0:T(8,128)}), f32[128,128]{1,0:T(8,128)}) %all-reduce.7.cloned.1.call-update) | async-done | bytes 65552 | tf_op jit(solution)/shard_map/psum | solution.py:50
  246.1 0.0 copy-done.2
  246.1 0.0 copy-done.3
  246.1 0.9 fusion.14
  247.0 8.0 %fusion.8 = f32[128,1,4,128]{3,1,2,0:T(1,128)S(1)} fusion(bf16[128,4,128,128]{3,2,1,0:T(8,128)(2,1)} %param.8, bf16[128,128,1,1]{1,0,2,3:T(8,128)(2,1)S(1)} %get-tuple-element.7), kind=kOutput, calls=%fused_computation.25 | convolution fusion | flops 16777216 | bytes 17072128 | tf_op jit(solution)/shard_map/rsij,ri->rsj/dot_general | solution.py:17
  255.1 0.2 broadcast_multiply_fusion
  255.3 3.7 scatter_custom_fusion.1
  259.0 0.0 all-reduce.9.cloned.1.call-update
  259.0 0.0 all-reduce.11.cloned.1.call-start
  259.0 0.6 multiply_reduce_fusion.5
  259.6 180.1 %psum.67 = f32[]{:T(128)} all-reduce(f32[]{:T(128)} %multiply_reduce_fusion.5), channel_id=1, replica_groups=mesh['rows'=64,'feat'=2] {'rows'}, use_global_device_ids=true, to_apply=%region_9.11 | all-reduce | flops 1 | bytes 8 | tf_op jit(solution)/shard_map/psum | solution.py:23
  440.4 0.0 all-reduce.9.cloned.1.call-done
  440.4 4.7 multiply_reduce_fusion
  445.1 3.1 psum.69
  448.9 1.8 multiply_convert_fusion
  450.7 1.3 gather_fusion.1
  452.0 0.2 select_bitcast_fusion
  452.3 0.0 copy-start.1
  452.3 12.4 %fusion.4 = f32[128,4,1,128]{3,2,1,0:T(1,128)S(1)} fusion(bf16[128,4,128,128]{3,2,1,0:T(8,128)(2,1)} %param.8, bf16[128,4,128,1]{2,1,0,3:T(4,128)(2,1)S(1)} %select_bitcast_fusion), kind=kOutput, calls=%fused_computation.15 | convolution fusion | flops 16777216 | bytes 17170432 | tf_op jit(solution)/shard_map/rsij,rsj->rsi/dot_general | solution.py:46
  464.6 0.9 multiply_reduce_fusion.2
  465.5 0.0 all-reduce.11.cloned.1.call-update
  465.8 16.6 %all-reduce.11.cloned.1.call-done = f32[128,128]{1,0:T(8,128)} async-done(((f32[128,128]{1,0:T(8,128)}), f32[128,128]{1,0:T(8,128)}) %all-reduce.11.cloned.1.call-update) | async-done | bytes 65552 | tf_op jit(solution)/shard_map/psum | solution.py:50
  482.4 2.1 multiply_reduce_fusion.4
  484.5 179.6 %psum.71 = f32[]{:T(128)} all-reduce(f32[]{:T(128)} %get-tuple-element.3), channel_id=1, replica_groups=mesh['rows'=64,'feat'=2] {'rows'}, use_global_device_ids=true, to_apply=%region_17.19 | all-reduce | flops 1 | bytes 8 | tf_op jit(solution)/shard_map/psum | solution.py:23
  664.9 0.0 copy-done.1
  664.9 3.4 multiply_add_fusion
  (2 shorter events, 0.0 us)
Async XLA Ops:
  7.2 197.8 %all-reduce.5.cloned.1.call-start = ((), (), s32[]{:S(2)}) async-start(), calls=%async_computation | async-start | bytes 4194304 | tf_op jit(solution)/shard_map/psum | solution.py:24
  18.6 186.3 %copy-start = (f32[4096,128]{1,0:T(8,128)S(1)}, f32[4096,128]{1,0:T(8,128)}, u32[]{:S(2)}) copy-start(f32[4096,128]{1,0:T(8,128)} %param.13) | copy-start | bytes 6291460
  22.3 223.8 %all-reduce.7.cloned.1.call-start = ((), (), s32[]{:S(2)}) async-start(), calls=%async_computation.1 | async-start | bytes 131072 | tf_op jit(solution)/shard_map/psum | solution.py:50
  216.1 30.0 %copy-start.2 = (f32[128,128]{1,0:T(8,128)S(1)}, f32[128,128]{1,0:T(8,128)}, u32[]{:S(2)}) copy-start(f32[128,128]{1,0:T(8,128)} %param.12) | copy-start | bytes 196612
  216.1 30.0 %copy-start.3 = (s32[128,128]{1,0:T(8,128)S(1)}, s32[128,128]{1,0:T(8,128)}, u32[]{:S(2)}) copy-start(s32[128,128]{1,0:T(8,128)} %param.11) | copy-start | bytes 196612
  229.3 211.1 %all-reduce.9.cloned.1.call-start = ((), (), s32[]{:S(2)}) async-start(), calls=%async_computation.2 | async-start | bytes 4194304 | tf_op jit(solution)/shard_map/psum | solution.py:24
  259.0 223.4 %all-reduce.11.cloned.1.call-start = ((), (), s32[]{:S(2)}) async-start(), calls=%async_computation.3 | async-start | bytes 131072 | tf_op jit(solution)/shard_map/psum | solution.py:50
  452.3 212.6 %copy-start.1 = (f32[4096,128]{1,0:T(8,128)S(1)}, f32[4096,128]{1,0:T(8,128)}, u32[]{:S(2)}) copy-start(f32[4096,128]{1,0:T(8,128)} %get-tuple-element.12) | copy-start | bytes 6291460
Sparse Core Ops, SparseCore 0:
  22.4 135.0 all-reduce.4
  229.4 16.6 all-reduce.6
  259.1 133.9 all-reduce.8
  465.7 16.6 all-reduce.10
where the time goes:
time: 675 us
  blocking collectives  547 us (81%)
  matrix products  40.7 us (6%)
  waiting for transfers between devices  33.3 us (5%)
  other arithmetic  32.2 us (5%)
  between operations  17.7 us (3%)
    psum x3, blocking collectives, backward(): squares = lax.psum(local_sq, 'rows')  541 us
    psum x2, waiting for transfers between devices, body(): lax.psum(forward_partial_value, 'feat')  33.2 us
    dot_general x2, matrix products, body(): jnp.einsum('rsij,rsj->rsi', blocks, picked, preferred_element_type=jnp.fl...  24.6 us
    dot_general x2, matrix products, backward(): jnp.einsum('rsij,ri->rsj', blocks, rowed, preferred_element_type=jnp.floa...  16.1 us
  transfers between devices with their start and end apart: 4, of which 2 were waited for; matrix products, arithmetic and copies ran while one was open for 0% of the time, Pallas kernels for 0%

commit v1 on v0

v1 whole, which is shorter than its diff:
```python
import functools

import jax
import jax.numpy as jnp
from jax import lax
from jax.experimental import pallas as pl
from jax.experimental.pallas import tpu as pltpu
from jax.sharding import PartitionSpec as P

F32 = jnp.float32
BF16 = jnp.bfloat16
EPS = 1e-06
META = 8
CHUNK = 16


def spread(value):
    full = jnp.broadcast_to(value, (META, 128))
    high = full.astype(BF16).astype(F32)
    rest = full - high
    mid = rest.astype(BF16).astype(F32)
    low = (rest - mid).astype(BF16).astype(F32)
    row = lax.broadcasted_iota(jnp.int32, (META, 128), 0)
    tile = jnp.where(row == 0, high, jnp.where(row == 1, mid, jnp.where(row == 2, low, 0.0)))
    return tile.astype(BF16)


def total_sum(x):
    return jnp.sum(jnp.sum(x, axis=0, keepdims=True), axis=1, keepdims=True)


def gathered_sum(tile):
    return jnp.sum(tile, axis=0, keepdims=True)[:, 0:1]


def backward_steps(own, blk, col, cnt, grow, tots, out, square):
    step = pl.program_id(0)
    feat_local = tots[0].shape[0]
    peers = out.shape[0]
    first = lax.axis_index("feat") * feat_local
    for rr in range(CHUNK):
        r = step * CHUNK + rr
        g = grow[pl.ds(r, 1), :].astype(BF16)
        n = cnt[r, 0]
        for s in range(blk.shape[1]):
            t = jnp.dot(g, blk[rr, s], preferred_element_type=F32)
            t = jnp.where(s < n, t, 0.0)
            tot = tots[s % len(tots)]
            c = col[r, s] - first
            tot[pl.ds(c, 1), :] += t

    @pl.when(step == pl.num_programs(0) - 1)
    def _():
        tile = spread(square[0:1, 0:1])

        def put(d, carry):
            at = pl.ds(pl.multiple_of(d * own, own), own)
            acc = tots[0][at, :]
            for tot in tots[1:]:
                acc = acc + tot[at, :]
            out[d, 0:own, :] = acc.astype(BF16)
            out[d, own : own + META, :] = tile
            return carry

        lax.fori_loop(0, peers, put, 0)


def clear(own, tots, peers):
    def zero(d, carry):
        at = pl.ds(pl.multiple_of(d * own, own), own)
        for tot in tots:
            tot[at, :] = jnp.zeros((own, 128), F32)
        return carry

    lax.fori_loop(0, peers, zero, 0)


def rhs_of(labels, weight):
    return weight[...] * (2 * labels[...] - 1).astype(F32)


def first_backward(own, col, cnt, labels, weight, blk, out, grow, square, *tots):
    @pl.when(pl.program_id(0) == 0)
    def _():
        resid = rhs_of(labels, weight)
        grow[...] = (weight[...] * resid).astype(BF16).astype(F32)
        square[...] = jnp.broadcast_to(total_sum(resid * resid), square.shape)
        clear(own, tots, out.shape[0])

    backward_steps(own, blk, col, cnt, grow, tots, out, square)


def next_backward(own, col, cnt, labels, weight, mine, other, scal, blk, out, resid_out, alpha_out, grow, square, *tots):
    @pl.when(pl.program_id(0) == 0)
    def _():
        rows = weight.shape[0]
        alpha = jnp.sqrt(gathered_sum(mine[rows:, :] + other[rows:, :]) + EPS)
        beta = scal[0:1, 0:1]
        unit = rhs_of(labels, weight) / beta
        resid = weight[...] * ((mine[0:rows, :] + other[0:rows, :]) / alpha) - alpha * unit
        resid_out[...] = resid
        alpha_out[...] = jnp.broadcast_to(alpha, alpha_out.shape)
        grow[...] = (weight[...] * resid).astype(BF16).astype(F32)
        square[...] = jnp.broadcast_to(total_sum(resid * resid), square.shape)
        clear(own, tots, out.shape[0])

    backward_steps(own, blk, col, cnt, grow, tots, out, square)


def reduced(own, recv):
    def add(d, carry):
        acc, meta = carry
        return acc + recv[d, 0:own, :].astype(F32), meta + recv[d, own : own + META, :].astype(F32)

    acc, meta = lax.fori_loop(
        0, recv.shape[0], add, (jnp.zeros((own, 128), F32), jnp.zeros((META, 128), F32)), unroll=8
    )
    return acc, jnp.sqrt(gathered_sum(meta) + EPS)


def send_step(own, out, step_vec):
    data = step_vec.astype(BF16)
    tile = spread(total_sum(step_vec * step_vec))

    def put(d, carry):
        out[d, 0:own, :] = data
        out[d, own : own + META, :] = tile
        return carry

    lax.fori_loop(0, out.shape[0], put, 0, unroll=8)


def first_owner(own, recv, scale_hbm, out, step_out, beta_out, scale, sem):
    start = pl.multiple_of(lax.axis_index("rows") * own, own)
    copy = pltpu.make_async_copy(scale_hbm.at[pl.ds(start, own), :], scale, sem)
    copy.start()
    total, beta = reduced(own, recv)
    copy.wait()
    step_vec = scale[...] * total / beta
    step_out[...] = step_vec
    beta_out[...] = jnp.broadcast_to(beta, beta_out.shape)
    send_step(own, out, step_vec)


def next_owner(own, recv, step_in, alpha_in, scale_hbm, out, beta_out, scale, sem):
    start = pl.multiple_of(lax.axis_index("rows") * own, own)
    copy = pltpu.make_async_copy(scale_hbm.at[pl.ds(start, own), :], scale, sem)
    copy.start()
    total, beta = reduced(own, recv)
    copy.wait()
    unit = step_in[...] / alpha_in[0:1, 0:1]
    step_vec = scale[...] * total / beta - beta * unit
    beta_out[...] = jnp.broadcast_to(beta, beta_out.shape)
    send_step(own, out, step_vec)


def forward(own, col, cnt, recv, scale, blk, out, table):
    step = pl.program_id(0)
    rows = out.shape[0] - META
    first = lax.axis_index("feat") * table.shape[0]

    @pl.when(step == 0)
    def _():
        def fill(d, meta):
            at = pl.ds(pl.multiple_of(d * own, own), own)
            scaled = scale[at, :] * recv[d, 0:own, :].astype(F32)
            table[at, :] = scaled.astype(BF16).astype(F32)
            return meta + recv[d, own : own + META, :].astype(F32)

        out[rows:, :] = lax.fori_loop(0, recv.shape[0], fill, jnp.zeros((META, 128), F32))

    for rr in range(CHUNK):
        r = step * CHUNK + rr
        n = cnt[r, 0]
        acc = jnp.zeros((1, 128), F32)
        for s in range(blk.shape[1]):
            c = col[r, s] - first
            v = jnp.where(s < n, table[pl.ds(c, 1), :], 0.0).astype(BF16)
            acc = acc + lax.dot_general(v, blk[rr, s], (((1,), (1,)), ((), ())), preferred_element_type=F32)
        out[pl.ds(r, 1), :] = acc


def last_rows(labels, weight, mine, other, resid_in, alpha_in, beta_in, resid_out, alpha_out, out):
    del labels
    rows = weight.shape[0]
    alpha = jnp.sqrt(gathered_sum(mine[rows:, :] + other[rows:, :]) + EPS)
    unit = resid_in[...] / beta_in[0:1, 0:1]
    resid = weight[...] * ((mine[0:rows, :] + other[0:rows, :]) / alpha) - alpha * unit
    resid_out[...] = resid
    alpha_out[...] = jnp.broadcast_to(alpha, alpha_out.shape)
    out[...] = jnp.broadcast_to(total_sum(resid * resid), out.shape)


def combine(own, recv0, recv1, squares, beta0, alpha0, beta1, alpha1, out):
    b0, a0 = beta0[0:1, 0:1], alpha0[0:1, 0:1]
    b1, a1 = beta1[0:1, 0:1], alpha1[0:1, 0:1]
    b2 = jnp.sqrt(jnp.sum(squares[...], axis=0, keepdims=True)[:, 0:1] + EPS)
    rho1 = jnp.sqrt(a0 * a0 + b1 * b1)
    cos1, sin1 = a0 / rho1, b1 / rho1
    theta1, bar1 = sin1 * a1, -cos1 * a1
    phi1, phibar1 = cos1 * b0, sin1 * b0
    rho2 = jnp.sqrt(bar1 * bar1 + b2 * b2)
    phi2 = (bar1 / rho2) * phibar1
    second = phi2 / rho2
    first = phi1 / rho1 - second * (theta1 / rho1)
    first, second = first / a0, second / a1
    for d in range(recv0.shape[0]):
        out[d * own : (d + 1) * own, :] = first * recv0[d, 0:own, :].astype(F32) + second * recv1[d, 0:own, :].astype(F32)


def body(blocks, col_index, row_counts, labels, row_weight, feature_scale):
    rows, slots, side, _ = blocks.shape
    feat_local = feature_scale.shape[0]
    peers = lax.axis_size("rows")
    own = feat_local // peers
    steps = rows // CHUNK
    smem = pl.BlockSpec(memory_space=pltpu.SMEM)
    vmem = pl.BlockSpec(memory_space=pltpu.VMEM)
    hbm = pl.BlockSpec(memory_space=pl.ANY)

    def whole(*shape):
        return pl.BlockSpec(shape, lambda i: (0,) * len(shape))

    blk = pl.BlockSpec((CHUNK, slots, side, side), lambda i: (i, 0, 0, 0))
    small = jax.ShapeDtypeStruct((8, 128), F32)
    rowvec = jax.ShapeDtypeStruct((rows, side), F32)
    packet = jax.ShapeDtypeStruct((peers, own + META, side), BF16)
    part = jax.ShapeDtypeStruct((rows + META, side), F32)
    params = pltpu.CompilerParams(vmem_limit_bytes=40 << 20)
    scratch = [pltpu.VMEM((rows, side), F32), pltpu.VMEM((8, 128), F32)]
    scratch += [pltpu.VMEM((feat_local, side), F32)] * slots
    scale_scratch = [pltpu.VMEM((own, side), F32), pltpu.SemaphoreType.DMA]

    def exchange(x):
        return lax.all_to_all(x, "rows", 0, 0)

    def swap(x):
        return lax.ppermute(x, "feat", [(0, 1), (1, 0)])

    def forward_part(recv):
        return pl.pallas_call(
            functools.partial(forward, own),
            grid=(steps,),
            out_shape=part,
            in_specs=[smem, smem, whole(*packet.shape), whole(feat_local, side), blk],
            out_specs=whole(*part.shape),
            scratch_shapes=[pltpu.VMEM((feat_local, side), F32)],
            compiler_params=params,
            name="forward",
        )(col_index, row_counts, recv, feature_scale, blocks)

    send = pl.pallas_call(
        functools.partial(first_backward, own),
        grid=(steps,),
        out_shape=packet,
        in_specs=[smem, smem, whole(rows, side), whole(rows, side), blk],
        out_specs=whole(*packet.shape),
        scratch_shapes=scratch,
        compiler_params=params,
        name="backward0",
    )(col_index, row_counts, labels, row_weight, blocks)
    send, step0, beta0 = pl.pallas_call(
        functools.partial(first_owner, own),
        out_shape=(packet, jax.ShapeDtypeStruct((own, side), F32), small),
        in_specs=[vmem, hbm],
        out_specs=(vmem, vmem, vmem),
        scratch_shapes=scale_scratch,
        compiler_params=params,
        name="owner0",
    )(exchange(send), feature_scale)
    recv0 = exchange(send)
    mine = forward_part(recv0)
    send, resid1, alpha0 = pl.pallas_call(
        functools.partial(next_backward, own),
        grid=(steps,),
        out_shape=(packet, rowvec, small),
        in_specs=[smem, smem, whole(rows, side), whole(rows, side), whole(*part.shape), whole(*part.shape), whole(8, 128), blk],
        out_specs=(whole(*packet.shape), whole(rows, side), whole(8, 128)),
        scratch_shapes=scratch,
        compiler_params=params,
        name="backward1",
    )(col_index, row_counts, labels, row_weight, mine, swap(mine), beta0, blocks)
    send, beta1 = pl.pallas_call(
        functools.partial(next_owner, own),
        out_shape=(packet, small),
        in_specs=[vmem, vmem, vmem, hbm],
        out_specs=(vmem, vmem),
        scratch_shapes=scale_scratch,
        compiler_params=params,
        name="owner1",
    )(exchange(send), step0, alpha0, feature_scale)
    recv1 = exchange(send)
    mine = forward_part(recv1)
    resid2, alpha1, send = pl.pallas_call(
        last_rows,
        out_shape=(rowvec, small, jax.ShapeDtypeStruct((peers, side), F32)),
        in_specs=[vmem] * 7,
        out_specs=(vmem, vmem, vmem),
        compiler_params=params,
        name="last_rows",
    )(labels, row_weight, mine, swap(mine), resid1, alpha0, beta1)
    solution = pl.pallas_call(
        functools.partial(combine, own),
        out_shape=jax.ShapeDtypeStruct((feat_local, side), F32),
        in_specs=[vmem] * 7,
        out_specs=vmem,
        compiler_params=params,
        name="combine",
    )(recv0, recv1, exchange(send), beta0, alpha0, beta1, alpha1)
    return (solution, resid2)


def solution(mesh):
    return jax.shard_map(
        body,
        mesh=mesh,
        in_specs=(
            P("rows", "feat", None, None),
            P("rows", "feat"),
            P("rows", "feat"),
            P("rows", None),
            P("rows", None),
            P("feat", None),
        ),
        out_specs=(P("feat", None), P("rows", None)),
        check_vma=False,
    )
```

time: 675 us -> 182 us (0.27)
  blocking collectives: 547 us -> 117 us
  Pallas kernels: 0 us -> 57.6 us
  matrix products: 40.7 us -> 0 us
  other arithmetic: 32.2 us -> 0 us
  waiting for transfers between devices: 33.3 us -> 2.54 us
  between operations: 17.7 us -> 0.7 us
    psum x5 -> x0, blocking collectives: 547 us -> none  [the longest x3 541 us: backward(): squares = lax.psum(local_sq, 'rows')]
    all_to_all x0 -> x5, blocking collectives: none -> 117 us  [exchange(): return lax.all_to_all(x, 'rows', 0, 0)]
    pallas_call x0 -> x8, Pallas kernels: none -> 57.6 us  [the longest x2 28.6 us: forward_part(): pl.pallas_call(functools.partial(forward, own), grid=(steps,), out_shape=...]
    dot_general x4 -> x0, matrix products: 40.7 us -> none  [the longest x2 24.6 us: body(): jnp.einsum('rsij,rsj->rsi', blocks, picked, preferred_element_type=jnp.fl...]
    psum x4 -> x0, waiting for transfers between devices: 33.2 us -> none  [the longest x2 33.2 us: body(): lax.psum(forward_partial_value, 'feat')]
    reduce_sum x6 -> x0, other arithmetic: 13.2 us -> none  [the longest x2 8.64 us: feat_norm(): local_sq = jnp.sum(step_vec * step_vec)]
    scatter-add x2 -> x0, other arithmetic: 7.33 us -> none  [backward(): jax.ops.segment_sum(terms.reshape(-1, block_side), local_col.reshape(-1),...]
    convert_element_type x5 -> x0, other arithmetic: 6.78 us -> none  [the longest x2 3.67 us: body(): scaled = (feature_scale * unit_feat).astype(jnp.bfloat16)]
  transfers between devices with their start and end apart: 4 -> 2, of which waited for: 2 -> 2; matrix products, arithmetic and copies ran while one was open for 0% -> 0% of each run, Pallas kernels for 0% -> 0%
where the time goes in v1:
time: 182 us
  blocking collectives  117 us (64%)
  Pallas kernels  57.6 us (32%)
  local copies, waits for them, and re-layouts  3.24 us (2%)
  waiting for transfers between devices  2.54 us (1%)
    all_to_all x5, blocking collectives, exchange(): return lax.all_to_all(x, 'rows', 0, 0)  117 us
    pallas_call x2, Pallas kernels, forward_part(): pl.pallas_call(functools.partial(forward, own), grid=(steps,), out_shape=...  28.6 us
    pallas_call x1, Pallas kernels, body(): pl.pallas_call(functools.partial(next_backward, own), grid=(steps,), out_...  12.8 us
    pallas_call x1, Pallas kernels, body(): pl.pallas_call(functools.partial(first_backward, own), grid=(steps,), out...  12.7 us
  transfers between devices with their start and end apart: 2, of which 2 were waited for; matrix products, arithmetic and copies ran while one was open for 0% of the time, Pallas kernels for 0%

profile of v1, /device:TPU:0, one launch (start us, length us, event | category | flops | bytes accessed | tf_op | source)
XLA Modules:
  0.0 181.5 jit_solution(16957005518823904262)
XLA Ops:
  0.6 0.8 copy.16.col
  1.4 0.8 copy.17.cnt
  2.2 0.0 copy-start.1
  2.2 0.8 copy-done.1
  3.0 0.0 copy-start.3
  3.0 0.8 copy-done.3
  3.9 12.7 %backward0.1 = bf16[64,72,128]{2,1,0:T(8,128)(2,1)S(1)} custom-call(s32[128,4]{1,0:T(8,128)S(1)} %copy.16.col, s32[128,1]{1,0:T(8,128)S(1)} %copy.17.cnt, s32[128,128]{1,0:T(8,128)S(1)} %copy-done.1, f32[128,128]{1,0:T(8,128)S(1)} %copy-done.3, bf16[128,4,128,128]{3,2,1,0:T(8,128)(2,1)} %blk.7), custom_call_target="tpu_custom_call" | custom-call | tf_op jit(solution)/shard_map/backward0/pallas_call | solution.py:252
  16.6 0.0 copy-start
  16.6 31.5 %all_to_all.31.recv = bf16[64,72,128]{2,1,0:T(8,128)(2,1)S(1)} all-to-all(bf16[64,72,128]{2,1,0:T(8,128)(2,1)S(1)} %backward0.1), channel_id=1, replica_groups=mesh['rows'=64,'feat'=2] {'rows'}, dimensions={0} | all-to-all | bytes 2359296 | tf_op jit(solution)/shard_map/all_to_all | solution.py:235
  48.1 0.0 copy-done
  48.1 0.5 owner0.1
  48.6 23.4 %all_to_all.32.recv.recv0 = bf16[64,72,128]{2,1,0:T(8,128)(2,1)S(1)} all-to-all(bf16[64,72,128]{2,1,0:T(8,128)(2,1)S(1)} %get-tuple-element.13), channel_id=1, replica_groups=mesh['rows'=64,'feat'=2] {'rows'}, dimensions={0} | all-to-all | bytes 2359296 | tf_op jit(solution)/shard_map/all_to_all | solution.py:235
  72.0 0.0 copy-start.2
  72.0 0.0 copy-start.4
  72.0 14.3 %forward.2.mine = f32[136,128]{1,0:T(8,128)S(1)} custom-call(s32[128,4]{1,0:T(8,128)S(1)} %copy.16.col, s32[128,1]{1,0:T(8,128)S(1)} %copy.17.cnt, bf16[64,72,128]{2,1,0:T(8,128)(2,1)S(1)} %all_to_all.32.recv.recv0, f32[4096,128]{1,0:T(8,128)S(1)} %copy-done, bf16[128,4,128,128]{3,2,1,0:T(8,128)(2,1)} %blk.7), custom_call_target="tpu_custom_call" | custom-call | tf_op jit(solution)/shard_map/forward/pallas_call | solution.py:241
  86.3 0.0 collective-permute-start
  86.4 1.3 collective-permute-done.other
  87.6 0.0 copy-done.2
  87.6 0.0 copy-done.4
  87.6 12.8 %backward1.1 = (bf16[64,72,128]{2,1,0:T(8,128)(2,1)S(1)}, f32[128,128]{1,0:T(8,128)S(1)}, f32[8,128]{1,0:T(8,128)S(1)}) custom-call(s32[128,4]{1,0:T(8,128)S(1)} %copy.16.col, s32[128,1]{1,0:T(8,128)S(1)} %copy.17.cnt, s32[128,128]{1,0:T(8,128)S(1)} %copy-done.2, f32[128,128]{1,0:T(8,128)S(1)} %copy-done.4, f32[136,128]{1,0:T(8,128)S(1)} %forward.2.mine, ...), custom_call_target="tpu_custom_call" | custom-call | tf_op jit(solution)/shard_map/backward1/pallas_call | solution.py:273
  100.5 24.9 %all_to_all.33.recv = bf16[64,72,128]{2,1,0:T(8,128)(2,1)S(1)} all-to-all(bf16[64,72,128]{2,1,0:T(8,128)(2,1)S(1)} %get-tuple-element.15), channel_id=1, replica_groups=mesh['rows'=64,'feat'=2] {'rows'}, dimensions={0} | all-to-all | bytes 2359296 | tf_op jit(solution)/shard_map/all_to_all | solution.py:235
  125.4 0.5 owner1.1
  125.9 23.5 %all_to_all.34.recv.recv1 = bf16[64,72,128]{2,1,0:T(8,128)(2,1)S(1)} all-to-all(bf16[64,72,128]{2,1,0:T(8,128)(2,1)S(1)} %get-tuple-element.18), channel_id=1, replica_groups=mesh['rows'=64,'feat'=2] {'rows'}, dimensions={0} | all-to-all | bytes 2359296 | tf_op jit(solution)/shard_map/all_to_all | solution.py:235
  149.4 14.3 %forward.3.mine = f32[136,128]{1,0:T(8,128)S(1)} custom-call(s32[128,4]{1,0:T(8,128)S(1)} %copy.16.col, s32[128,1]{1,0:T(8,128)S(1)} %copy.17.cnt, bf16[64,72,128]{2,1,0:T(8,128)(2,1)S(1)} %all_to_all.34.recv.recv1, f32[4096,128]{1,0:T(8,128)S(1)} %copy-done, bf16[128,4,128,128]{3,2,1,0:T(8,128)(2,1)} %blk.7), custom_call_target="tpu_custom_call" | custom-call | tf_op jit(solution)/shard_map/forward/pallas_call | solution.py:241
  163.7 0.0 collective-permute-start.1
  163.7 1.3 collective-permute-done.1.other
  165.0 0.7 last_rows.1
  165.8 14.1 %all_to_all.35 = f32[64,1,128]{2,1,0:T(1,128)S(1)} all-to-all(f32[64,1,128]{2,1,0:T(1,128)S(1)} %bitcast.5), channel_id=1, replica_groups=mesh['rows'=64,'feat'=2] {'rows'}, dimensions={0} | all-to-all | bytes 65536 | tf_op jit(solution)/shard_map/all_to_all | solution.py:235
  179.8 1.7 combine.1
Async XLA Ops:
  2.2 0.8 copy-start.1
  3.0 0.8 copy-start.3
  16.6 31.5 %copy-start = (f32[4096,128]{1,0:T(8,128)S(1)}, f32[4096,128]{1,0:T(8,128)}, u32[]{:S(2)}) copy-start(f32[4096,128]{1,0:T(8,128)} %scale.3) | copy-start | bytes 6291460
  72.0 15.6 %copy-start.2 = (s32[128,128]{1,0:T(8,128)S(1)}, s32[128,128]{1,0:T(8,128)}, u32[]{:S(2)}) copy-start(s32[128,128]{1,0:T(8,128)} %labels.5) | copy-start | bytes 196612
  72.0 15.6 %copy-start.4 = (f32[128,128]{1,0:T(8,128)S(1)}, f32[128,128]{1,0:T(8,128)}, u32[]{:S(2)}) copy-start(f32[128,128]{1,0:T(8,128)} %weight.5) | copy-start | bytes 196612
  86.3 1.3 collective-permute-start
  163.7 1.3 collective-permute-start.1

commit v2 on v1

v2 whole, which is shorter than its diff:
```python
import functools

import jax
import jax.numpy as jnp
from jax import lax
from jax.experimental import pallas as pl
from jax.experimental.pallas import tpu as pltpu
from jax.sharding import PartitionSpec as P

F32 = jnp.float32
BF16 = jnp.bfloat16
EPS = 1e-06
META = 8
UNROLL = 16
PHASES = 4
COPIES = 32
LIST = 640
TABLES = 4


def spread(value):
    full = jnp.broadcast_to(value, (META, 128))
    high = full.astype(BF16).astype(F32)
    rest = full - high
    mid = rest.astype(BF16).astype(F32)
    low = (rest - mid).astype(BF16).astype(F32)
    row = lax.broadcasted_iota(jnp.int32, (META, 128), 0)
    tile = jnp.where(row == 0, high, jnp.where(row == 1, mid, jnp.where(row == 2, low, 0.0)))
    return tile.astype(BF16)


def total_sum(x):
    return jnp.sum(jnp.sum(x, axis=0, keepdims=True), axis=1, keepdims=True)


def gathered_sum(tile):
    return jnp.sum(tile, axis=0, keepdims=True)[:, 0:1]


def build_list(col, cnt, codes, first):
    slots, rows = col.shape
    pad = rows << 12
    at = 0
    for p in range(PHASES):

        def row(r, k):
            n = cnt[0, r]
            for s in range(slots):
                codes[k] = (col[s, r] - first) | (r << 12) | ((r * slots + s) << 20)
                k = k + (s < n).astype(jnp.int32)
            return k

        at = lax.fori_loop(p * (rows // PHASES), (p + 1) * (rows // PHASES), row, at)
        for u in range(UNROLL):
            codes[at + u] = pad
        at = ((at + UNROLL - 1) // UNROLL) * UNROLL
        codes[LIST - 1 - p] = at


def decode(code):
    return code & 4095, (code >> 12) & 255, code >> 20


def tile_row(ref, i):
    return jnp.broadcast_to(ref[i >> 3, pl.ds(i & 7, 1), :], (8, 128))


def left_operand(parts, split):
    row = lax.broadcasted_iota(jnp.int32, (8, 128), 0)
    place = row & 3 if split else row
    halves = []
    for a, b in parts:
        x = jnp.where(place == a[0], a[1], jnp.where(place == b[0], b[1], 0.0))
        if split:
            high = x.astype(BF16).astype(F32)
            x = jnp.where(row < 4, high, x - high)
        halves.append(x.astype(BF16))
    return jnp.concatenate(halves, axis=1)


def right_operand(blk, e):
    top = jnp.concatenate([blk[e[0]], blk[e[1]]], axis=1)
    low = jnp.concatenate([blk[e[2]], blk[e[3]]], axis=1)
    return jnp.concatenate([top, low], axis=0)


def pick(t, m, half, split):
    lanes = slice(half * 128, half * 128 + 128)
    return t[m : m + 1, lanes] + t[m + 4 : m + 5, lanes] if split else t[m : m + 1, lanes]


def add_row(ref, i, value):
    ref[i >> 3, pl.ds(i & 7, 1), :] += value


def backward_range(codes, blk, grow, tots, begin, end, split):
    def some(i, carry):
        for q in range(UNROLL // 4):
            at = i * UNROLL + q * 4
            c, r, e = zip(*[decode(codes[at + u]) for u in range(4)])
            g = [tile_row(grow, r[u]) for u in range(4)]
            lhs = left_operand([((0, g[0]), (1, g[1])), ((2, g[2]), (3, g[3]))], split)
            t = jnp.dot(lhs, right_operand(blk, e), preferred_element_type=F32)
            for u in range(4):
                add_row(tots[u], c[u], pick(t, u, u & 1, split))
        return carry

    lax.fori_loop(begin // UNROLL, end // UNROLL, some, 0)


def forward_range(codes, blk, table, outs, begin, end):
    def some(i, carry):
        for q in range(UNROLL // 4):
            at = i * UNROLL + q * 4
            c, r, e = zip(*[decode(codes[at + u]) for u in range(4)])
            v = [tile_row(table, c[u]) for u in range(4)]
            lhs = left_operand([((0, v[0]), (2, v[2])), ((1, v[1]), (3, v[3]))], False)
            t = lax.dot_general(lhs, right_operand(blk, e), (((1,), (1,)), ((), ())), preferred_element_type=F32)
            for u in range(4):
                add_row(outs[u], r[u], pick(t, u, u >> 1, False))
        return carry

    lax.fori_loop(begin // UNROLL, end // UNROLL, some, 0)


def clear(refs):
    def zero(d, carry):
        for ref in refs:
            for u in range(8):
                ref[d * 8 + u] = jnp.zeros((8, 128), F32)
        return carry

    lax.fori_loop(0, refs[0].shape[0] // 8, zero, 0)


def set_rows(grow, value):
    rows = value.shape[0]
    grow[0 : rows // 8] = value.reshape(rows // 8, 8, 128)
    grow[rows // 8 :] = jnp.zeros((grow.shape[0] - rows // 8, 8, 128), F32)


def send_partials(own, tots, square, out):
    tile = spread(square)
    tiles = own // 8

    def put(d, carry):
        at = pl.ds(d * tiles, tiles)
        acc = tots[0][at]
        for tot in tots[1:]:
            acc = acc + tot[at]
        out[d, 0:own, :] = acc.reshape(own, 128).astype(BF16)
        out[d, own : own + META, :] = tile
        return carry

    lax.fori_loop(0, out.shape[0], put, 0)


def rhs_of(labels, weight):
    return weight[...] * (2 * labels[...] - 1).astype(F32)


def first_backward(own, col, cnt, labels_hbm, weight_hbm, blocks, out, held, codes, labels, weight, grow, sems, row_sems, *tots):
    slots = col.shape[0]
    each = held.shape[0] // COPIES
    copies = [
        pltpu.make_async_copy(blocks.at[pl.ds(i * each, each)], held.at[pl.ds(i * each, each)], sems.at[i]) for i in range(COPIES)
    ]
    small = [
        pltpu.make_async_copy(labels_hbm, labels, row_sems.at[0]),
        pltpu.make_async_copy(weight_hbm, weight, row_sems.at[1]),
    ]
    for copy in small + copies:
        copy.start()
    build_list(col, cnt, codes, lax.axis_index("feat") * (tots[0].shape[0] * 8))
    clear(tots)
    for copy in small:
        copy.wait()
    resid = rhs_of(labels, weight)
    set_rows(grow, (weight[...] * resid).astype(BF16).astype(F32))
    begin = 0
    for p in range(PHASES):
        for copy in copies[p * (COPIES // PHASES) : (p + 1) * (COPIES // PHASES)]:
            copy.wait()
        end = codes[LIST - 1 - p]
        backward_range(codes, held, grow, tots, begin, end, False)
        begin = end
    send_partials(own, tots, total_sum(resid * resid), out)


def next_backward(own, codes, labels, weight, mine, other, beta_in, held, out, resid_out, alpha_out, grow, *tots):
    rows = weight.shape[0]
    clear(tots)
    alpha = jnp.sqrt(gathered_sum(mine[rows:, :] + other[rows:, :]) + EPS)
    unit = rhs_of(labels, weight) / beta_in[0:1, 0:1]
    resid = weight[...] * ((mine[0:rows, :] + other[0:rows, :]) / alpha) - alpha * unit
    resid_out[...] = resid
    alpha_out[...] = jnp.broadcast_to(alpha, alpha_out.shape)
    set_rows(grow, weight[...] * resid)
    backward_range(codes, held, grow, tots, 0, codes[LIST - PHASES], True)
    send_partials(own, tots, total_sum(resid * resid), out)


def reduced(own, recv):
    def add(d, carry):
        acc, meta = carry
        return acc + recv[d, 0:own, :].astype(F32), meta + recv[d, own : own + META, :].astype(F32)

    acc, meta = lax.fori_loop(
        0, recv.shape[0], add, (jnp.zeros((own, 128), F32), jnp.zeros((META, 128), F32)), unroll=8
    )
    return acc, jnp.sqrt(gathered_sum(meta) + EPS)


def send_step(own, out, step_vec, scale):
    data = (scale * step_vec).astype(BF16)
    tile = spread(total_sum(step_vec * step_vec))

    def put(d, carry):
        out[d, 0:own, :] = data
        out[d, own : own + META, :] = tile
        return carry

    lax.fori_loop(0, out.shape[0], put, 0, unroll=8)


def first_owner(own, recv, scale_hbm, out, step_out, beta_out, scale, sem):
    start = pl.multiple_of(lax.axis_index("rows") * own, own)
    copy = pltpu.make_async_copy(scale_hbm.at[pl.ds(start, own), :], scale, sem)
    copy.start()
    total, beta = reduced(own, recv)
    copy.wait()
    step_vec = scale[...] * total / beta
    step_out[...] = step_vec
    beta_out[...] = jnp.broadcast_to(beta, beta_out.shape)
    send_step(own, out, step_vec, scale[...])


def next_owner(own, recv, step_in, alpha_in, scale_hbm, out, beta_out, scale, sem):
    start = pl.multiple_of(lax.axis_index("rows") * own, own)
    copy = pltpu.make_async_copy(scale_hbm.at[pl.ds(start, own), :], scale, sem)
    copy.start()
    total, beta = reduced(own, recv)
    copy.wait()
    unit = step_in[...] / alpha_in[0:1, 0:1]
    step_vec = scale[...] * total / beta - beta * unit
    beta_out[...] = jnp.broadcast_to(beta, beta_out.shape)
    send_step(own, out, step_vec, scale[...])


def forward(own, codes, recv, held, out, table, *outs):
    rows = out.shape[0] - META
    tiles = own // 8

    def fill(d, meta):
        table[pl.ds(d * tiles, tiles)] = recv[d, 0:own, :].astype(F32).reshape(tiles, 8, 128)
        return meta + recv[d, own : own + META, :].astype(F32)

    out[rows:, :] = lax.fori_loop(0, recv.shape[0], fill, jnp.zeros((META, 128), F32))
    for ref in outs:
        ref[...] = jnp.zeros_like(ref)
    forward_range(codes, held, table, outs, 0, codes[LIST - PHASES])
    acc = outs[0][0 : rows // 8]
    for ref in outs[1:]:
        acc = acc + ref[0 : rows // 8]
    out[0:rows, :] = acc.reshape(rows, 128)


def last_rows(weight, mine, other, resid_in, beta_in, resid_out, alpha_out, out):
    rows = weight.shape[0]
    alpha = jnp.sqrt(gathered_sum(mine[rows:, :] + other[rows:, :]) + EPS)
    unit = resid_in[...] / beta_in[0:1, 0:1]
    resid = weight[...] * ((mine[0:rows, :] + other[0:rows, :]) / alpha) - alpha * unit
    resid_out[...] = resid
    alpha_out[...] = jnp.broadcast_to(alpha, alpha_out.shape)
    out[...] = jnp.broadcast_to(total_sum(resid * resid), out.shape)


def combine(own, recv0, recv1, scale, squares, beta0, alpha0, beta1, alpha1, out):
    b0, a0 = beta0[0:1, 0:1], alpha0[0:1, 0:1]
    b1, a1 = beta1[0:1, 0:1], alpha1[0:1, 0:1]
    b2 = jnp.sqrt(jnp.sum(squares[...], axis=0, keepdims=True)[:, 0:1] + EPS)
    rho1 = jnp.sqrt(a0 * a0 + b1 * b1)
    cos1, sin1 = a0 / rho1, b1 / rho1
    theta1, bar1 = sin1 * a1, -cos1 * a1
    phi1, phibar1 = cos1 * b0, sin1 * b0
    rho2 = jnp.sqrt(bar1 * bar1 + b2 * b2)
    phi2 = (bar1 / rho2) * phibar1
    second = phi2 / rho2
    first = phi1 / rho1 - second * (theta1 / rho1)
    first, second = first / a0, second / a1

    def put(d, carry):
        at = pl.ds(pl.multiple_of(d * own, own), own)
        mixed = first * recv0[d, 0:own, :].astype(F32) + second * recv1[d, 0:own, :].astype(F32)
        out[at, :] = mixed / scale[at, :]
        return carry

    lax.fori_loop(0, recv0.shape[0], put, 0, unroll=2)


def body(blocks, col_index, row_counts, labels, row_weight, feature_scale):
    rows, slots, side, _ = blocks.shape
    feat_local = feature_scale.shape[0]
    peers = lax.axis_size("rows")
    own = feat_local // peers
    far = [pltpu.with_memory_space_constraint(x, pltpu.HBM) for x in (col_index.T, row_counts.T, labels, row_weight)]
    far_blocks = pltpu.with_memory_space_constraint(blocks.reshape(rows * slots, side, side), pltpu.HBM)
    smem = pl.BlockSpec(memory_space=pltpu.SMEM)
    vmem = pl.BlockSpec(memory_space=pltpu.VMEM)
    hbm = pl.BlockSpec(memory_space=pltpu.HBM)
    small = jax.ShapeDtypeStruct((8, 128), F32)
    rowvec = jax.ShapeDtypeStruct((rows, side), F32)
    packet = jax.ShapeDtypeStruct((peers, own + META, side), BF16)
    part = jax.ShapeDtypeStruct((rows + META, side), F32)
    params = pltpu.CompilerParams(vmem_limit_bytes=20 << 20)
    tables = [pltpu.VMEM((feat_local // 8, 8, side), F32)] * TABLES
    row_table = pltpu.VMEM((rows // 8 + 1, 8, side), F32)
    scale_scratch = [pltpu.VMEM((own, side), F32), pltpu.SemaphoreType.DMA]

    def exchange(x):
        return lax.all_to_all(x, "rows", 0, 0)

    def swap(x):
        return lax.ppermute(x, "feat", [(0, 1), (1, 0)])

    def forward_part(recv):
        return pl.pallas_call(
            functools.partial(forward, own),
            out_shape=part,
            in_specs=[smem, vmem, vmem],
            out_specs=vmem,
            scratch_shapes=[tables[0]] + [row_table] * TABLES,
            compiler_params=params,
            name="forward",
        )(codes, recv, held)

    send, held, codes = pl.pallas_call(
        functools.partial(first_backward, own),
        out_shape=(packet, pltpu.VMEM((rows * slots, side, side), BF16), jax.ShapeDtypeStruct((LIST,), jnp.int32)),
        in_specs=[smem, smem, hbm, hbm, hbm],
        out_specs=(vmem, vmem, smem),
        scratch_shapes=[
            pltpu.VMEM((rows, side), jnp.int32),
            pltpu.VMEM((rows, side), F32),
            row_table,
            pltpu.SemaphoreType.DMA((COPIES,)),
            pltpu.SemaphoreType.DMA((2,)),
        ]
        + tables,
        compiler_params=params,
        name="backward0",
    )(*far, far_blocks)
    send, step0, beta0 = pl.pallas_call(
        functools.partial(first_owner, own),
        out_shape=(packet, jax.ShapeDtypeStruct((own, side), F32), small),
        in_specs=[vmem, hbm],
        out_specs=(vmem, vmem, vmem),
        scratch_shapes=scale_scratch,
        compiler_params=params,
        name="owner0",
    )(exchange(send), feature_scale)
    recv0 = exchange(send)
    mine = forward_part(recv0)
    send, resid1, alpha0 = pl.pallas_call(
        functools.partial(next_backward, own),
        out_shape=(packet, rowvec, small),
        in_specs=[smem] + [vmem] * 6,
        out_specs=(vmem, vmem, vmem),
        scratch_shapes=[row_table] + tables,
        compiler_params=params,
        name="backward1",
    )(codes, labels, row_weight, mine, swap(mine), beta0, held)
    send, beta1 = pl.pallas_call(
        functools.partial(next_owner, own),
        out_shape=(packet, small),
        in_specs=[vmem, vmem, vmem, hbm],
        out_specs=(vmem, vmem),
        scratch_shapes=scale_scratch,
        compiler_params=params,
        name="owner1",
    )(exchange(send), step0, alpha0, feature_scale)
    recv1 = exchange(send)
    mine = forward_part(recv1)
    resid2, alpha1, send = pl.pallas_call(
        last_rows,
        out_shape=(rowvec, small, jax.ShapeDtypeStruct((peers, side), F32)),
        in_specs=[vmem] * 5,
        out_specs=(vmem, vmem, vmem),
        compiler_params=params,
        name="last_rows",
    )(row_weight, mine, swap(mine), resid1, beta1)
    solution = pl.pallas_call(
        functools.partial(combine, own),
        out_shape=jax.ShapeDtypeStruct((feat_local, side), F32),
        in_specs=[vmem] * 8,
        out_specs=vmem,
        compiler_params=params,
        name="combine",
    )(recv0, recv1, feature_scale, exchange(send), beta0, alpha0, beta1, alpha1)
    return (solution, resid2)


def solution(mesh):
    return jax.shard_map(
        body,
        mesh=mesh,
        in_specs=(
            P("rows", "feat", None, None),
            P("rows", "feat"),
            P("rows", "feat"),
            P("rows", None),
            P("rows", None),
            P("feat", None),
        ),
        out_specs=(P("feat", None), P("rows", None)),
        check_vma=False,
    )
```

time: 182 us -> 159 us (0.87)
  Pallas kernels: 57.6 us -> 36.9 us
  local copies, waits for them, and re-layouts: 3.24 us -> 0.01 us
    pallas_call x4, Pallas kernels: 54.2 us -> 32.3 us  [the longest x2 13.5 us: forward_part(): pl.pallas_call(functools.partial(forward, own), out_shape=part, in_specs=...]
    unnamed x12 -> x6, local copies, waits for them, and re-layouts: 3.24 us -> 0.01 us
where the time goes in v2:
time: 159 us; the launch traced here: 158 us
  blocking collectives  118 us (74%)
  Pallas kernels  36.9 us (23%)
  waiting for transfers between devices  2.49 us (2%)
    all_to_all x5, blocking collectives, exchange(): return lax.all_to_all(x, 'rows', 0, 0)  118 us
    pallas_call x2, Pallas kernels, forward_part(): pl.pallas_call(functools.partial(forward, own), out_shape=part, in_specs=...  13.5 us
    pallas_call x1, Pallas kernels, body(): pl.pallas_call(functools.partial(first_backward, own), out_shape=(packet,...  12.4 us
    pallas_call x1, Pallas kernels, body(): pl.pallas_call(functools.partial(next_backward, own), out_shape=(packet,...  6.44 us
  transfers between devices with their start and end apart: 2, of which 2 were waited for; matrix products, arithmetic and copies ran while one was open for 0% of the time, Pallas kernels for 0%

profile of v2, /device:TPU:0, one launch (start us, length us, event | category | flops | bytes accessed | tf_op | source)
XLA Modules:
  0.0 158.3 jit_solution(11858340065997696775)
XLA Ops:
  0.6 12.4 %backward0.1 = (bf16[64,72,128]{2,1,0:T(8,128)(2,1)S(1)}, bf16[512,128,128]{2,1,0:T(8,128)(2,1)S(1)}, s32[640]{0:T(1024)S(1)}) custom-call(s32[4,128]{1,0:T(4,128)} %bitcast.10, s32[1,128]{1,0:T(1,128)} %bitcast.11, s32[128,128]{1,0:T(8,128)} %labels.1, f32[128,128]{1,0:T(8,128)} %weight.3, bf16[512,128,128]{2,1,0:T(8,128)(2,1)} %bitcast.9), custom_call_target="tpu_custom_call" | custom-call | tf_op jit(solution)/shard_map/backward0/pallas_call | solution.py:337
  13.0 0.0 copy-start
  13.0 31.5 %all_to_all.31.recv = bf16[64,72,128]{2,1,0:T(8,128)(2,1)S(1)} all-to-all(bf16[64,72,128]{2,1,0:T(8,128)(2,1)S(1)} %get-tuple-element.16), channel_id=1, replica_groups=mesh['rows'=64,'feat'=2] {'rows'}, dimensions={0} | all-to-all | bytes 2359296 | tf_op jit(solution)/shard_map/all_to_all | solution.py:321
  44.6 0.0 copy-done
  44.6 0.5 owner0.1
  45.1 23.2 %all_to_all.32.recv.recv0 = bf16[64,72,128]{2,1,0:T(8,128)(2,1)S(1)} all-to-all(bf16[64,72,128]{2,1,0:T(8,128)(2,1)S(1)} %get-tuple-element.17), channel_id=1, replica_groups=mesh['rows'=64,'feat'=2] {'rows'}, dimensions={0} | all-to-all | bytes 2359296 | tf_op jit(solution)/shard_map/all_to_all | solution.py:321
  68.3 0.0 copy-start.1
  68.3 0.0 copy-start.2
  68.3 6.7 %forward.2.mine = f32[136,128]{1,0:T(8,128)S(1)} custom-call(s32[640]{0:T(1024)S(1)} %get-tuple-element.18.codes, bf16[64,72,128]{2,1,0:T(8,128)(2,1)S(1)} %all_to_all.32.recv.recv0, bf16[512,128,128]{2,1,0:T(8,128)(2,1)S(1)} %get-tuple-element.19.held), custom_call_target="tpu_custom_call" | custom-call | tf_op jit(solution)/shard_map/forward/pallas_call | solution.py:327
  75.0 0.1 collective-permute-start
  75.1 1.2 collective-permute-done.other
  76.4 0.0 copy-done.1
  76.4 0.0 copy-done.2
  76.4 6.4 %backward1.1 = (bf16[64,72,128]{2,1,0:T(8,128)(2,1)S(1)}, f32[128,128]{1,0:T(8,128)S(1)}, f32[8,128]{1,0:T(8,128)S(1)}) custom-call(s32[640]{0:T(1024)S(1)} %get-tuple-element.18.codes, s32[128,128]{1,0:T(8,128)S(1)} %copy-done.2, f32[128,128]{1,0:T(8,128)S(1)} %copy-done.1, f32[136,128]{1,0:T(8,128)S(1)} %forward.2.mine, ...), custom_call_target="tpu_custom_call" | custom-call | tf_op jit(solution)/shard_map/backward1/pallas_call | solution.py:364
  82.8 25.5 %all_to_all.33.recv = bf16[64,72,128]{2,1,0:T(8,128)(2,1)S(1)} all-to-all(bf16[64,72,128]{2,1,0:T(8,128)(2,1)S(1)} %get-tuple-element.21), channel_id=1, replica_groups=mesh['rows'=64,'feat'=2] {'rows'}, dimensions={0} | all-to-all | bytes 2359296 | tf_op jit(solution)/shard_map/all_to_all | solution.py:321
  108.3 0.5 owner1.1
  108.8 23.4 %all_to_all.34.recv.recv1 = bf16[64,72,128]{2,1,0:T(8,128)(2,1)S(1)} all-to-all(bf16[64,72,128]{2,1,0:T(8,128)(2,1)S(1)} %get-tuple-element.24), channel_id=1, replica_groups=mesh['rows'=64,'feat'=2] {'rows'}, dimensions={0} | all-to-all | bytes 2359296 | tf_op jit(solution)/shard_map/all_to_all | solution.py:321
  132.3 6.7 %forward.3.mine = f32[136,128]{1,0:T(8,128)S(1)} custom-call(s32[640]{0:T(1024)S(1)} %get-tuple-element.18.codes, bf16[64,72,128]{2,1,0:T(8,128)(2,1)S(1)} %all_to_all.34.recv.recv1, bf16[512,128,128]{2,1,0:T(8,128)(2,1)S(1)} %get-tuple-element.19.held), custom_call_target="tpu_custom_call" | custom-call | tf_op jit(solution)/shard_map/forward/pallas_call | solution.py:327
  139.0 0.1 collective-permute-start.1
  139.1 1.2 collective-permute-done.1.other
  140.3 0.7 last_rows.1
  141.1 14.4 %all_to_all.35 = f32[64,1,128]{2,1,0:T(1,128)S(1)} all-to-all(f32[64,1,128]{2,1,0:T(1,128)S(1)} %bitcast.8), channel_id=1, replica_groups=mesh['rows'=64,'feat'=2] {'rows'}, dimensions={0} | all-to-all | bytes 65536 | tf_op jit(solution)/shard_map/all_to_all | solution.py:321
  155.5 2.8 %combine.1 = f32[4096,128]{1,0:T(8,128)} custom-call(bf16[64,72,128]{2,1,0:T(8,128)(2,1)S(1)} %all_to_all.32.recv.recv0, bf16[64,72,128]{2,1,0:T(8,128)(2,1)S(1)} %all_to_all.34.recv.recv1, f32[4096,128]{1,0:T(8,128)S(1)} %copy-done, f32[64,128]{1,0:T(8,128)S(1)} %bitcast.7, f32[8,128]{1,0:T(8,128)S(1)} %get-tuple-element.20.beta_in.beta0, ...), custom_call_target="tpu_custom_call" | custom-call | tf_op jit(solution)/shard_map/combine/pallas_call | solution.py:392
Async XLA Ops:
  13.0 31.5 %copy-start = (f32[4096,128]{1,0:T(8,128)S(1)}, f32[4096,128]{1,0:T(8,128)}, u32[]{:S(2)}) copy-start(f32[4096,128]{1,0:T(8,128)} %scale.1) | copy-start | bytes 6291460
  68.3 8.1 %copy-start.1 = (f32[128,128]{1,0:T(8,128)S(1)}, f32[128,128]{1,0:T(8,128)}, u32[]{:S(2)}) copy-start(f32[128,128]{1,0:T(8,128)} %weight.3) | copy-start | bytes 196612
  68.3 8.1 %copy-start.2 = (s32[128,128]{1,0:T(8,128)S(1)}, s32[128,128]{1,0:T(8,128)}, u32[]{:S(2)}) copy-start(s32[128,128]{1,0:T(8,128)} %labels.1) | copy-start | bytes 196612
  75.0 1.3 collective-permute-start
  139.0 1.3 collective-permute-start.1

commit v3 on v2

v3 whole, which is shorter than its diff:
```python
import functools

import jax
import jax.numpy as jnp
from jax import lax
from jax.experimental import pallas as pl
from jax.experimental.pallas import tpu as pltpu
from jax.sharding import PartitionSpec as P

F32 = jnp.float32
BF16 = jnp.bfloat16
EPS = 1e-06
ITERS = 2
META = 8
UNROLL = 32
COPIES = 32
EARLY = 8
LIST = 640
TABLES = 4
PACKET = 32
ROOM = PACKET - 1
RAISED = 128.0


def spread(value):
    full = jnp.broadcast_to(value, (META, 128))
    high = full.astype(BF16).astype(F32)
    rest = full - high
    mid = rest.astype(BF16).astype(F32)
    low = (rest - mid).astype(BF16).astype(F32)
    row = lax.broadcasted_iota(jnp.int32, (META, 128), 0)
    tile = jnp.where(row == 0, high, jnp.where(row == 1, mid, jnp.where(row == 2, low, 0.0)))
    return tile.astype(BF16)


def total_sum(x):
    return jnp.sum(jnp.sum(x, axis=0, keepdims=True), axis=1, keepdims=True)


def gathered_sum(tile):
    return jnp.sum(tile, axis=0, keepdims=True)[:, 0:1]


def decode(code):
    return code & 4095, (code >> 12) & 255, code >> 20


def tile_row(ref, i):
    return jnp.broadcast_to(ref[i >> 3, pl.ds(i & 7, 1), :], (8, 128))


def left_operand(parts, split):
    row = lax.broadcasted_iota(jnp.int32, (8, 128), 0)
    place = row & 3 if split else row
    halves = []
    for a, b in parts:
        x = jnp.where(place == a[0], a[1], jnp.where(place == b[0], b[1], 0.0))
        if split:
            high = x.astype(BF16).astype(F32)
            x = jnp.where(row < 4, high, x - high)
        halves.append(x.astype(BF16))
    return jnp.concatenate(halves, axis=1)


def right_operand(blk, e):
    top = jnp.concatenate([blk[e[0]], blk[e[1]]], axis=1)
    low = jnp.concatenate([blk[e[2]], blk[e[3]]], axis=1)
    return jnp.concatenate([top, low], axis=0)


def pick(t, m, half, split):
    lanes = slice(half * 128, half * 128 + 128)
    return t[m : m + 1, lanes] + t[m + 4 : m + 5, lanes] if split else t[m : m + 1, lanes]


def put_row(ref, i, value):
    ref[i >> 3, pl.ds(i & 7, 1), :] = value


def add_row(ref, i, value):
    ref[i >> 3, pl.ds(i & 7, 1), :] += value


def backward_list(codes, blk, grow, stage):
    def some(i, carry):
        for q in range(UNROLL // 4):
            at = i * UNROLL + q * 4
            c, r, e = zip(*[decode(codes[at + u]) for u in range(4)])
            g = [tile_row(grow, r[u]) for u in range(4)]
            lhs = left_operand([((0, g[0]), (1, g[1])), ((2, g[2]), (3, g[3]))], True)
            t = jnp.dot(lhs, right_operand(blk, e), preferred_element_type=F32)
            for u in range(4):
                put_row(stage, c[u], pick(t, u, u & 1, True))
        return carry

    lax.fori_loop(0, codes[LIST - 1] // UNROLL, some, 0)


def forward_list(codes, blk, table, outs):
    def some(i, carry):
        for q in range(UNROLL // 4):
            at = i * UNROLL + q * 4
            c, r, e = zip(*[decode(codes[at + u]) for u in range(4)])
            v = [tile_row(table, c[u]) for u in range(4)]
            lhs = left_operand([((0, v[0]), (2, v[2])), ((1, v[1]), (3, v[3]))], False)
            t = lax.dot_general(lhs, right_operand(blk, e), (((1,), (1,)), ((), ())), preferred_element_type=F32)
            for u in range(4):
                add_row(outs[u], r[u], pick(t, u, u >> 1, False))
        return carry

    lax.fori_loop(0, codes[LIST - 1] // UNROLL, some, 0)


def clear(ref):
    def zero(d, carry):
        ref[d] = jnp.zeros((8, 128), F32)
        return carry

    lax.fori_loop(0, ref.shape[0], zero, 0, unroll=8)


def set_rows(grow, value):
    rows = value.shape[0]
    grow[0 : rows // 8] = value.reshape(rows // 8, 8, 128)
    grow[rows // 8 :] = jnp.zeros((grow.shape[0] - rows // 8, 8, 128), F32)


def quarter():
    lane = lax.broadcasted_iota(jnp.int32, (8, 128), 1) // (128 // 4)
    return (lane - lax.axis_index("rows")) & 3


def send_partials(stage, index, meta, square, flag, out):
    part = quarter()
    lane = lax.broadcasted_iota(jnp.int32, (8, 128), 1)
    three = spread(square).astype(F32)
    sums = jnp.where(part == 1, three[0:1, :], jnp.where(part == 2, three[1:2, :], three[2:3, :]))
    raised = (part == 0) & (lane % PACKET == ROOM)
    for d in range(index.shape[0]):
        meta[d] = jnp.where(part != 0, sums, jnp.where(raised, flag, index[d]))
    tiles = PACKET // 8
    last = lax.broadcasted_iota(jnp.int32, (PACKET, 128), 0) == ROOM

    def put(d, carry):
        row = jnp.broadcast_to(meta[d >> 3, pl.ds(d & 7, 1), :], (PACKET, 128))
        rows = stage[pl.ds(d * tiles, tiles)].reshape(PACKET, 128)
        out[d] = jnp.where(last, row, rows).astype(BF16)
        return carry

    lax.fori_loop(0, out.shape[0], put, 0, unroll=4)


def rhs_of(labels, weight):
    return weight[...] * (2 * labels[...] - 1).astype(F32)


def place_entries(own, peers, cols, counts, places, index):
    slots, rows = cols.shape
    first = lax.axis_index("feat") * (own * peers)
    lane0 = (lax.axis_index("rows") & 3) * PACKET
    owner_id = lax.broadcasted_iota(jnp.int32, (peers, rows), 0)
    down = lax.broadcasted_iota(jnp.int32, (rows, rows), 0)
    earlier = jnp.where(down < lax.broadcasted_iota(jnp.int32, (rows, rows), 1), 1.0, 0.0).astype(BF16)
    before = jnp.zeros((peers, 1), F32)
    meta = jnp.zeros((peers, rows), F32)
    for s in range(slots):
        c = cols[s : s + 1, :] - first
        owner = lax.shift_right_logical(c, own.bit_length() - 1)
        live = s < counts[...]
        hit = jnp.where((owner_id == owner) & live, 1.0, 0.0)
        rank = before + jnp.dot(hit.astype(BF16), earlier, preferred_element_type=F32)
        before = before + jnp.sum(hit, axis=1, keepdims=True)
        rank = jnp.sum(hit * rank, axis=0, keepdims=True).astype(jnp.int32)
        fits = live & (rank < ROOM)
        places[s : s + 1, :] = jnp.where(fits, owner * PACKET + rank, peers * PACKET)
        lane = jnp.where(fits, rank + lane0, -1)
        known = ((c & (own - 1)) + 1).astype(F32)
        spot = jnp.where(down == lane, 1.0, 0.0).astype(BF16)
        meta = meta + lax.dot_general(
            (hit * known).astype(BF16), spot, (((1,), (1,)), ((), ())), preferred_element_type=F32
        )
    index[...] = meta.reshape(index.shape)
    return jnp.where(jnp.max(before, axis=0, keepdims=True) > ROOM, RAISED, 0.0)


def first_backward(
    own, col_hbm, cnt_hbm, labels_hbm, weight_hbm, blocks, out, held, forth, back, index,
    cols, counts, col, cnt, places, labels, weight, wide, place_tile, stage, meta, sems, small_sems,
):
    slots, rows = cols.shape
    each = held.shape[0] // COPIES
    per_step = 8 * slots // each
    first = lax.axis_index("feat") * (own * out.shape[0])

    def block_copy(i):
        at = pl.ds(i * each, each)
        return pltpu.make_async_copy(blocks.at[at], held.at[at], sems.at[i])

    pairs = ((col_hbm, cols), (cnt_hbm, counts), (labels_hbm, labels), (weight_hbm, weight), (col_hbm, col), (cnt_hbm, cnt))
    small = [pltpu.make_async_copy(src, dst, small_sems.at[i]) for i, (src, dst) in enumerate(pairs)]
    for copy in small:
        copy.start()
    for i in range(EARLY):
        block_copy(i).start()
    clear(stage)
    for copy in small:
        copy.wait()
    flag = place_entries(own, out.shape[0], cols, counts, place_tile, index)
    to_scalars = pltpu.make_async_copy(place_tile, places, small_sems.at[len(pairs)])
    to_scalars.start(priority=1)
    for i in range(EARLY, COPIES):
        block_copy(i).start()
    resid = rhs_of(labels, weight)
    rowed = (weight[...] * resid).astype(BF16).astype(F32)
    odd = lax.broadcasted_iota(jnp.int32, rowed.shape, 0) & 1
    wide[:, 0:128] = jnp.where(odd == 0, rowed, 0.0)
    wide[:, 128:256] = jnp.where(odd == 1, rowed, 0.0)
    to_scalars.wait()

    def step(p, k):
        r0 = pl.multiple_of(p * 8, 8)
        for i in range(per_step):
            block_copy(p * per_step + i).wait()
        lhs = wide[pl.ds(r0, 8), :].astype(BF16)
        for pair in range(4):
            for h in range(slots // 2):
                e = [(r0 + 2 * pair + q) * slots + 2 * h + s for q in range(2) for s in range(2)]
                t = jnp.dot(lhs, right_operand(held, e), preferred_element_type=F32)
                for u in range(4):
                    m, slot = 2 * pair + u // 2, 2 * h + u % 2
                    r = r0 + m
                    place = places[slot, r]
                    put_row(stage, place, pick(t, m, u % 2, False))
                    code = (r << 12) | (e[u] << 20)
                    forth[k] = code | (col[slot, r] - first)
                    back[k] = code | place
                    k = k + (slot < cnt[0, r]).astype(jnp.int32)
        return k

    live = lax.fori_loop(0, rows // 8, step, 0)
    for u in range(UNROLL):
        forth[live + u] = rows << 12
        back[live + u] = (rows << 12) | (out.shape[0] * PACKET)
    end = ((live + UNROLL - 1) // UNROLL) * UNROLL
    forth[LIST - 1] = end
    back[LIST - 1] = end
    send_partials(stage, index, meta, total_sum(resid * resid), flag, out)


def next_backward(codes, labels, weight, mine, other, scal, index, held, out, resid_out, scal_out, grow, stage, meta):
    rows = weight.shape[0]
    clear(stage)
    both = mine[rows:, :] + other[rows:, :]
    alpha = jnp.sqrt(gathered_sum(both[0:3, :]) + EPS)
    unit = rhs_of(labels, weight) / scal[0:1, 0:1]
    resid = weight[...] * ((mine[0:rows, :] + other[0:rows, :]) / alpha) - alpha * unit
    resid_out[...] = resid
    scal_out[...] = pair_tile(alpha, both[3:4, 0:1])
    set_rows(grow, weight[...] * resid)
    backward_list(codes, held, grow, stage)
    send_partials(stage, index, meta, total_sum(resid * resid), 0.0, out)


def pair_tile(a, b):
    row = lax.broadcasted_iota(jnp.int32, (8, 128), 0)
    return jnp.where(row == 0, jnp.broadcast_to(a, (8, 128)), jnp.broadcast_to(b, (8, 128)))


def reduced(own, recv):
    lane = lax.broadcasted_iota(jnp.int32, (1, 128), 1) // PACKET
    feature = (lax.broadcasted_iota(jnp.int32, (own, 128), 0) + 1).astype(F32)
    acc = jnp.zeros((own, 128), F32)
    sums = jnp.zeros((1, 128), F32)
    most = jnp.zeros((1, 128), F32)
    for g in range(recv.shape[0] // 4):
        known = jnp.zeros((1, 128), F32)
        for j in range(4):
            row = recv[4 * g + j, PACKET - 8 : PACKET, :].astype(F32)[7:8, :]
            known = known + jnp.where(lane == j, row, 0.0)
            sums = sums + jnp.where(lane == j, 0.0, row)
        most = jnp.maximum(most, known)
        chosen = jnp.where(feature == known, 1.0, 0.0).astype(BF16)
        acc = acc + jnp.dot(chosen, recv[4 * g : 4 * g + 4].reshape(128, 128), preferred_element_type=F32)
    first = lax.broadcasted_iota(jnp.int32, (1, 128), 1) % PACKET == 0
    total = jnp.sum(jnp.where(first, sums, 0.0), axis=1, keepdims=True)
    return acc, jnp.sqrt(total + EPS), jnp.max(most, axis=1, keepdims=True)


def send_step(own, out, step_vec, scale):
    data = (scale * step_vec).astype(BF16)
    tile = spread(total_sum(step_vec * step_vec))

    def put(d, carry):
        out[d, 0:own, :] = data
        out[d, own : own + META, :] = tile
        return carry

    lax.fori_loop(0, out.shape[0], put, 0, unroll=8)


def first_owner(own, recv, scale_hbm, out, step_out, beta_out, scale, sem):
    start = pl.multiple_of(lax.axis_index("rows") * own, own)
    copy = pltpu.make_async_copy(scale_hbm.at[pl.ds(start, own), :], scale, sem)
    copy.start()
    total, beta, most = reduced(own, recv)
    copy.wait()
    step_vec = scale[...] * total / beta
    step_out[...] = step_vec
    beta_out[...] = pair_tile(beta, jnp.where(most > own, 1.0, 0.0))
    send_step(own, out, step_vec, scale[...])


def next_owner(own, recv, step_in, alpha_in, scale_hbm, out, beta_out, scale, sem):
    start = pl.multiple_of(lax.axis_index("rows") * own, own)
    copy = pltpu.make_async_copy(scale_hbm.at[pl.ds(start, own), :], scale, sem)
    copy.start()
    total, beta, _ = reduced(own, recv)
    copy.wait()
    unit = step_in[...] / alpha_in[0:1, 0:1]
    step_vec = scale[...] * total / beta - beta * unit
    beta_out[...] = jnp.broadcast_to(beta, beta_out.shape)
    send_step(own, out, step_vec, scale[...])


def forward(own, codes, recv, scal, held, out, table, *outs):
    rows = out.shape[0] - META
    tiles = own // 8

    def fill(d, meta):
        table[pl.ds(d * tiles, tiles)] = recv[d, 0:own, :].astype(F32).reshape(tiles, 8, 128)
        return meta + recv[d, own : own + META, :].astype(F32)

    meta = lax.fori_loop(0, recv.shape[0], fill, jnp.zeros((META, 128), F32), unroll=2)
    row = lax.broadcasted_iota(jnp.int32, (META, 128), 0)
    out[rows:, :] = jnp.where(row == 3, scal[1:2, :], meta)
    for ref in outs:
        ref[...] = jnp.zeros_like(ref)
    forward_list(codes, held, table, outs)
    acc = outs[0][0 : rows // 8]
    for ref in outs[1:]:
        acc = acc + ref[0 : rows // 8]
    out[0:rows, :] = acc.reshape(rows, 128)


def last_rows(weight, mine, other, resid_in, beta_in, resid_out, alpha_out, out):
    rows = weight.shape[0]
    both = mine[rows:, :] + other[rows:, :]
    alpha = jnp.sqrt(gathered_sum(both[0:3, :]) + EPS)
    unit = resid_in[...] / beta_in[0:1, 0:1]
    resid = weight[...] * ((mine[0:rows, :] + other[0:rows, :]) / alpha) - alpha * unit
    resid_out[...] = resid
    alpha_out[...] = jnp.broadcast_to(alpha, alpha_out.shape)
    out[...] = jnp.broadcast_to(total_sum(resid * resid), out.shape)


def combine(own, recv0, recv1, scale, squares, beta0, alpha0, beta1, alpha1, out_hbm, flag, out, sems):
    b0, a0 = beta0[0:1, 0:1], alpha0[0:1, 0:1]
    b1, a1 = beta1[0:1, 0:1], alpha1[0:1, 0:1]
    b2 = jnp.sqrt(jnp.sum(squares[...], axis=0, keepdims=True)[:, 0:1] + EPS)
    rho1 = jnp.sqrt(a0 * a0 + b1 * b1)
    cos1, sin1 = a0 / rho1, b1 / rho1
    theta1, bar1 = sin1 * a1, -cos1 * a1
    phi1, phibar1 = cos1 * b0, sin1 * b0
    rho2 = jnp.sqrt(bar1 * bar1 + b2 * b2)
    phi2 = (bar1 / rho2) * phibar1
    second = phi2 / rho2
    first = phi1 / rho1 - second * (theta1 / rho1)
    first, second = first / a0, second / a1
    flag[...] = jnp.broadcast_to(alpha0[1:2, :], flag.shape)
    n = sems.shape[0]
    each = out.shape[0] // n

    def copy(i):
        at = pl.ds(pl.multiple_of(i * each, each), each)
        return pltpu.make_async_copy(out.at[at], out_hbm.at[at], sems.at[i])

    def put(i, carry):
        for j in range(each // own):
            d = i * (each // own) + j
            at = pl.ds(pl.multiple_of(d * own, own), own)
            mixed = first * recv0[d, 0:own, :].astype(F32) + second * recv1[d, 0:own, :].astype(F32)
            out[at, :] = mixed / scale[at, :]
        copy(i).start()
        return carry

    lax.fori_loop(0, n, put, 0)
    lax.fori_loop(0, n, lambda i, carry: (copy(i).wait(), carry)[1], 0)


def general(blocks, col_index, row_counts, labels, row_weight, feature_scale):
    feat_local, side = feature_scale.shape
    peers = lax.axis_size("rows")
    local_col = col_index - lax.axis_index("feat") * feat_local
    live = (lax.broadcasted_iota(jnp.int32, col_index.shape, 1) < row_counts).astype(F32)

    def over_rows(x):
        return jnp.sum(lax.all_to_all(jnp.broadcast_to(x, (peers, 8, 128)), "rows", 0, 0), axis=0)[0, 0]

    def over_feat(x):
        return x + lax.ppermute(x, "feat", [(0, 1), (1, 0)])

    def backward(resid):
        rowed = (row_weight * resid).astype(BF16)
        terms = jnp.einsum("rsij,ri->rsj", blocks, rowed, preferred_element_type=F32) * live[:, :, None]
        partial = jax.ops.segment_sum(terms.reshape(-1, side), local_col.reshape(-1), num_segments=feat_local)
        owned = jnp.sum(lax.all_to_all(partial.reshape(peers, -1, side), "rows", 0, 0), axis=0)
        total = lax.all_to_all(jnp.broadcast_to(owned, (peers,) + owned.shape), "rows", 0, 0).reshape(feat_local, side)
        return total, jnp.sqrt(over_rows(jnp.sum(resid * resid)) + EPS)

    def norm(step_vec):
        return jnp.sqrt(over_feat(jnp.full((8, 128), jnp.sum(step_vec * step_vec)))[0, 0] + EPS)

    resid = row_weight * (2 * labels - 1).astype(F32)
    total, beta = backward(resid)
    step_vec = feature_scale * total / beta
    alpha = norm(step_vec)
    unit_feat = step_vec / alpha
    start = (resid, beta, alpha, unit_feat, beta, alpha, unit_feat, jnp.zeros_like(unit_feat))

    def iteration(_, state):
        resid, beta, alpha, unit_feat, phi_bar, rho_bar, search, result = state
        scaled = (feature_scale * unit_feat).astype(BF16)
        picked = jnp.take(scaled, local_col, axis=0)
        terms = jnp.einsum("rsij,rsj->rsi", blocks, picked, preferred_element_type=F32)
        resid = row_weight * over_feat(jnp.sum(terms * live[:, :, None], axis=1)) - alpha * (resid / beta)
        total, beta = backward(resid)
        step_vec = feature_scale * total / beta - beta * unit_feat
        alpha = norm(step_vec)
        unit_feat = step_vec / alpha
        rho = jnp.sqrt(rho_bar * rho_bar + beta * beta)
        cosine, sine = rho_bar / rho, beta / rho
        theta, rho_bar = sine * alpha, -cosine * alpha
        phi, phi_bar = cosine * phi_bar, sine * phi_bar
        result = result + phi / rho * search
        search = unit_feat - theta / rho * search
        return (resid, beta, alpha, unit_feat, phi_bar, rho_bar, search, result)

    state = lax.fori_loop(0, ITERS, iteration, start)
    return state[-1], state[0]


def body(blocks, col_index, row_counts, labels, row_weight, feature_scale):
    rows, slots, side, _ = blocks.shape
    feat_local = feature_scale.shape[0]
    peers = lax.axis_size("rows")
    own = feat_local // peers
    far = [pltpu.with_memory_space_constraint(x, pltpu.HBM) for x in (col_index.T, row_counts.T, labels, row_weight)]
    far_blocks = pltpu.with_memory_space_constraint(blocks.reshape(rows * slots, side, side), pltpu.HBM)
    smem = pl.BlockSpec(memory_space=pltpu.SMEM)
    vmem = pl.BlockSpec(memory_space=pltpu.VMEM)
    hbm = pl.BlockSpec(memory_space=pltpu.HBM)
    small = jax.ShapeDtypeStruct((8, 128), F32)
    rowvec = jax.ShapeDtypeStruct((rows, side), F32)
    packet = jax.ShapeDtypeStruct((peers, own + META, side), BF16)
    sparse = jax.ShapeDtypeStruct((peers, PACKET, side), BF16)
    part = jax.ShapeDtypeStruct((rows + META, side), F32)
    listed = jax.ShapeDtypeStruct((LIST,), jnp.int32)
    marked = jax.ShapeDtypeStruct((peers // 8, 8, side), F32)
    params = pltpu.CompilerParams(vmem_limit_bytes=20 << 20)
    table = pltpu.VMEM((feat_local // 8, 8, side), F32)
    stage = pltpu.VMEM((peers * PACKET // 8 + 1, 8, side), F32)
    mark = pltpu.VMEM(marked.shape, F32)
    row_table = pltpu.VMEM((rows // 8 + 1, 8, side), F32)
    scale_scratch = [pltpu.VMEM((own, side), F32), pltpu.SemaphoreType.DMA]

    def exchange(x):
        return lax.all_to_all(x, "rows", 0, 0)

    def swap(x):
        return lax.ppermute(x, "feat", [(0, 1), (1, 0)])

    def forward_part(recv, scal):
        return pl.pallas_call(
            functools.partial(forward, own),
            out_shape=part,
            in_specs=[smem, vmem, vmem, vmem],
            out_specs=vmem,
            scratch_shapes=[table] + [row_table] * TABLES,
            compiler_params=params,
            name="forward",
        )(forth, recv, scal, held)

    send, held, forth, back, index = pl.pallas_call(
        functools.partial(first_backward, own),
        out_shape=(
            sparse,
            pltpu.VMEM((rows * slots, side, side), BF16),
            listed,
            listed,
            marked,
        ),
        in_specs=[hbm] * 5,
        out_specs=(vmem, vmem, smem, smem, vmem),
        scratch_shapes=[
            pltpu.VMEM((slots, rows), jnp.int32),
            pltpu.VMEM((1, rows), jnp.int32),
            pltpu.SMEM((slots, rows), jnp.int32),
            pltpu.SMEM((1, rows), jnp.int32),
            pltpu.SMEM((slots, rows), jnp.int32),
            pltpu.VMEM((rows, side), jnp.int32),
            pltpu.VMEM((rows, side), F32),
            pltpu.VMEM((rows, 2 * side), F32),
            pltpu.VMEM((slots, rows), jnp.int32),
            stage,
            mark,
            pltpu.SemaphoreType.DMA((COPIES,)),
            pltpu.SemaphoreType.DMA((7,)),
        ],
        compiler_params=params,
        name="backward0",
    )(*far, far_blocks)
    send, step0, beta0 = pl.pallas_call(
        functools.partial(first_owner, own),
        out_shape=(packet, jax.ShapeDtypeStruct((own, side), F32), small),
        in_specs=[vmem, hbm],
        out_specs=(vmem, vmem, vmem),
        scratch_shapes=scale_scratch,
        compiler_params=params,
        name="owner0",
    )(exchange(send), feature_scale)
    recv0 = exchange(send)
    mine = forward_part(recv0, beta0)
    send, resid1, alpha0 = pl.pallas_call(
        next_backward,
        out_shape=(sparse, rowvec, small),
        in_specs=[smem] + [vmem] * 7,
        out_specs=(vmem, vmem, vmem),
        scratch_shapes=[row_table, stage, mark],
        compiler_params=params,
        name="backward1",
    )(back, labels, row_weight, mine, swap(mine), beta0, index, held)
    send, beta1 = pl.pallas_call(
        functools.partial(next_owner, own),
        out_shape=(packet, small),
        in_specs=[vmem, vmem, vmem, hbm],
        out_specs=(vmem, vmem),
        scratch_shapes=scale_scratch,
        compiler_params=params,
        name="owner1",
    )(exchange(send), step0, alpha0, feature_scale)
    recv1 = exchange(send)
    mine = forward_part(recv1, beta0)
    resid2, alpha1, send = pl.pallas_call(
        last_rows,
        out_shape=(rowvec, small, jax.ShapeDtypeStruct((peers, side), F32)),
        in_specs=[vmem] * 5,
        out_specs=(vmem, vmem, vmem),
        compiler_params=params,
        name="last_rows",
    )(row_weight, mine, swap(mine), resid1, beta1)
    result, flag = pl.pallas_call(
        functools.partial(combine, own),
        out_shape=(jax.ShapeDtypeStruct((feat_local, side), F32), small),
        in_specs=[vmem] * 8,
        out_specs=(hbm, vmem),
        scratch_shapes=[pltpu.VMEM((feat_local, side), F32), pltpu.SemaphoreType.DMA((16,))],
        compiler_params=params,
        name="combine",
    )(recv0, recv1, feature_scale, exchange(send), beta0, alpha0, beta1, alpha1)

    def fits(state):
        return state[0] > 0.0

    def again(state):
        args = (blocks, col_index, row_counts, labels, row_weight, feature_scale)
        return (jnp.zeros_like(state[0]),) + general(*lax.optimization_barrier((state[0],) + args)[1:])

    _, result, resid2 = lax.while_loop(fits, again, (flag[0, 0], result, resid2))
    return (result, resid2)


def solution(mesh):
    return jax.shard_map(
        body,
        mesh=mesh,
        in_specs=(
            P("rows", "feat", None, None),
            P("rows", "feat"),
            P("rows", "feat"),
            P("rows", None),
            P("rows", None),
            P("feat", None),
        ),
        out_specs=(P("feat", None), P("rows", None)),
        check_vma=False,
    )
```

time: 159 us -> 138 us (0.87)
  blocking collectives: 118 us -> 88.8 us
  waiting for transfers between devices: 2.49 us -> 11.2 us
  Pallas kernels: 36.9 us -> 29.6 us
  starting transfers between devices: 0.17 us -> 5.14 us
    all_to_all x5 -> x4, blocking collectives: 118 us -> 88.8 us  [exchange(): return lax.all_to_all(x, 'rows', 0, 0)]
    all_to_all x0 -> x1, waiting for transfers between devices: none -> 8.73 us  [exchange(): return lax.all_to_all(x, 'rows', 0, 0)]
    all_to_all x0 -> x1, starting transfers between devices: none -> 4.97 us  [exchange(): return lax.all_to_all(x, 'rows', 0, 0)]
    pallas_call x3, Pallas kernels: 21.7 us -> 17.2 us  [the longest x1 9.31 us: body(): pl.pallas_call(functools.partial(first_backward, own), out_shape=(sparse,...]
    pallas_call x2, Pallas kernels: 13.5 us -> 10.5 us  [forward_part(): pl.pallas_call(functools.partial(forward, own), out_shape=part, in_specs=...]
  transfers between devices with their start and end apart: 2 -> 3, of which waited for: 2 -> 3; matrix products, arithmetic and copies ran while one was open for 0% -> 1% of each run, Pallas kernels for 0% -> 0%
where the time goes in v3:
time: 138 us
  blocking collectives  88.8 us (64%)
  Pallas kernels  29.6 us (21%)
  waiting for transfers between devices  11.2 us (8%)
  starting transfers between devices  5.14 us (4%)
    all_to_all x4, blocking collectives, exchange(): return lax.all_to_all(x, 'rows', 0, 0)  88.8 us
    pallas_call x2, Pallas kernels, forward_part(): pl.pallas_call(functools.partial(forward, own), out_shape=part, in_specs=...  10.5 us
    pallas_call x1, Pallas kernels, body(): pl.pallas_call(functools.partial(first_backward, own), out_shape=(sparse,...  9.31 us
    all_to_all x1, waiting for transfers between devices, exchange(): return lax.all_to_all(x, 'rows', 0, 0)  8.73 us
    all_to_all x1, starting transfers between devices, exchange(): return lax.all_to_all(x, 'rows', 0, 0)  4.97 us
    pallas_call x1, Pallas kernels, body(): pl.pallas_call(next_backward, out_shape=(sparse, rowvec, small), in_specs...  4.43 us
    pallas_call x1, Pallas kernels, body(): pl.pallas_call(functools.partial(combine, own), out_shape=(jax.ShapeDtype...  3.49 us
  transfers between devices with their start and end apart: 3, of which 3 were waited for; matrix products, arithmetic and copies ran while one was open for 1% of the time, Pallas kernels for 0%

profile of v3, /device:TPU:0, one launch (start us, length us, event | category | flops | bytes accessed | tf_op | source)
XLA Modules:
  0.0 137.7 jit_solution(3455091127575516782)
XLA Ops:
  0.6 0.0 copy-start
  0.6 9.3 %backward0.1 = (bf16[64,32,128]{2,1,0:T(8,128)(2,1)S(1)}, bf16[512,128,128]{2,1,0:T(8,128)(2,1)S(1)}, s32[640]{0:T(1024)S(1)}, s32[640]{0:T(1024)S(1)}, f32[8,8,128]{2,1,0:T(8,128)S(1)}) custom-call(s32[4,128]{1,0:T(4,128)} %bitcast.102, s32[1,128]{1,0:T(1,128)} %bitcast.98, s32[128,128]{1,0:T(8,128)} %labels.1, f32[128,128]{1,0:T(8,128)} %weight.3, ...), custom_call_target="tpu_custom_call" | custom-call | tf_op jit(solution)/shard_map/backward0/pallas_call | solution.py:483
  10.0 24.6 %all_to_all.70.recv = bf16[64,32,128]{2,1,0:T(8,128)(2,1)S(1)} all-to-all(bf16[64,32,128]{2,1,0:T(8,128)(2,1)S(1)} %get-tuple-element.177), channel_id=1, replica_groups=mesh['rows'=64,'feat'=2] {'rows'}, dimensions={0} | all-to-all | bytes 1048576 | tf_op jit(solution)/shard_map/all_to_all | solution.py:467
  34.5 0.0 copy-done
  34.5 0.5 owner0.1
  35.0 23.2 %all_to_all.71.recv.recv0 = bf16[64,72,128]{2,1,0:T(8,128)(2,1)S(1)} all-to-all(bf16[64,72,128]{2,1,0:T(8,128)(2,1)S(1)} %get-tuple-element.178), channel_id=1, replica_groups=mesh['rows'=64,'feat'=2] {'rows'}, dimensions={0} | all-to-all | bytes 2359296 | tf_op jit(solution)/shard_map/all_to_all | solution.py:467
  58.2 0.0 copy-start.4
  58.2 5.2 %forward.2.mine = f32[136,128]{1,0:T(8,128)S(1)} custom-call(s32[640]{0:T(1024)S(1)} %get-tuple-element.180.codes, bf16[64,72,128]{2,1,0:T(8,128)(2,1)S(1)} %all_to_all.71.recv.recv0, f32[8,128]{1,0:T(8,128)S(1)} %get-tuple-element.181.scal.beta0, bf16[512,128,128]{2,1,0:T(8,128)(2,1)S(1)} %get-tuple-element.182.held), custom_call_target="tpu_custom_call" | custom-call | tf_op jit(solution)/shard_map/forward/pallas_call | solution.py:473
  63.5 0.1 collective-permute-start.3
  63.6 1.2 collective-permute-done.3.other
  64.8 0.0 copy-done.4
  64.8 4.4 %backward1.1 = (bf16[64,32,128]{2,1,0:T(8,128)(2,1)S(1)}, f32[128,128]{1,0:T(8,128)S(1)}, f32[8,128]{1,0:T(8,128)S(1)}) custom-call(s32[640]{0:T(1024)S(1)} %get-tuple-element.179.codes, s32[128,128]{1,0:T(8,128)} %labels.1, f32[128,128]{1,0:T(8,128)S(1)} %copy-done.4, f32[136,128]{1,0:T(8,128)S(1)} %forward.2.mine, ...), custom_call_target="tpu_custom_call" | custom-call | tf_op jit(solution)/shard_map/backward1/pallas_call | solution.py:523
  69.3 18.1 %all_to_all.72.recv = bf16[64,32,128]{2,1,0:T(8,128)(2,1)S(1)} all-to-all(bf16[64,32,128]{2,1,0:T(8,128)(2,1)S(1)} %get-tuple-element.184), channel_id=1, replica_groups=mesh['rows'=64,'feat'=2] {'rows'}, dimensions={0} | all-to-all | bytes 1048576 | tf_op jit(solution)/shard_map/all_to_all | solution.py:467
  87.4 0.5 owner1.1
  87.9 23.0 %all_to_all.73.recv.recv1 = bf16[64,72,128]{2,1,0:T(8,128)(2,1)S(1)} all-to-all(bf16[64,72,128]{2,1,0:T(8,128)(2,1)S(1)} %get-tuple-element.187), channel_id=1, replica_groups=mesh['rows'=64,'feat'=2] {'rows'}, dimensions={0} | all-to-all | bytes 2359296 | tf_op jit(solution)/shard_map/all_to_all | solution.py:467
  110.9 0.0 copy-start.6
  110.9 5.2 %forward.3.mine = f32[136,128]{1,0:T(8,128)S(1)} custom-call(s32[640]{0:T(1024)S(1)} %get-tuple-element.180.codes, bf16[64,72,128]{2,1,0:T(8,128)(2,1)S(1)} %all_to_all.73.recv.recv1, f32[8,128]{1,0:T(8,128)S(1)} %get-tuple-element.181.scal.beta0, bf16[512,128,128]{2,1,0:T(8,128)(2,1)S(1)} %get-tuple-element.182.held), custom_call_target="tpu_custom_call" | custom-call | tf_op jit(solution)/shard_map/forward/pallas_call | solution.py:473
  116.1 0.1 collective-permute-start.4
  116.2 1.2 collective-permute-done.4.other
  117.5 0.8 last_rows.1
  118.3 5.0 %all-to-all-start.10 = ((f32[64,1,128]{2,1,0:T(1,128)}), f32[64,1,128]{2,1,0:T(1,128)S(1)}, u32[]{:S(2)}, u32[]{:S(2)}) async-start(f32[64,1,128]{2,1,0:T(1,128)} %bitcast.13), calls=%async_computation.10 | async-start | bytes 65536 | tf_op jit(solution)/shard_map/all_to_all | solution.py:467
  123.3 0.0 copy-done.6
  123.3 0.7 copy.16
  124.0 8.7 %all-to-all-done.10 = f32[64,1,128]{2,1,0:T(1,128)S(1)} async-done(((f32[64,1,128]{2,1,0:T(1,128)}), f32[64,1,128]{2,1,0:T(1,128)S(1)}, u32[]{:S(2)}, u32[]{:S(2)}) %all-to-all-start.10) | async-done | bytes 32800 | tf_op jit(solution)/shard_map/all_to_all | solution.py:467
  132.7 0.0 copy-start.5
  132.7 3.5 %combine.1 = (f32[4096,128]{1,0:T(8,128)}, f32[8,128]{1,0:T(8,128)S(1)}) custom-call(bf16[64,72,128]{2,1,0:T(8,128)(2,1)S(1)} %all_to_all.71.recv.recv0, bf16[64,72,128]{2,1,0:T(8,128)(2,1)S(1)} %all_to_all.73.recv.recv1, f32[4096,128]{1,0:T(8,128)} %scale.1, f32[64,128]{1,0:T(8,128)S(1)} %bitcast.86, f32[8,128]{1,0:T(8,128)S(1)} %get-tuple-element.181.scal.beta0, ...), custom_call_target="tpu_custom_call" | custom-call | tf_op jit(solution)/shard_map/combine/pallas_call | solution.py:551
  136.2 0.5 slice.17
  136.7 0.0 copy-done.5
  136.7 0.8 while.36
Async XLA Ops:
  0.6 33.9 %copy-start = (f32[4096,128]{1,0:T(8,128)S(1)}, f32[4096,128]{1,0:T(8,128)}, u32[]{:S(2)}) copy-start(f32[4096,128]{1,0:T(8,128)} %scale.1) | copy-start | bytes 6291460
  58.2 6.6 %copy-start.4 = (f32[128,128]{1,0:T(8,128)S(1)}, f32[128,128]{1,0:T(8,128)}, u32[]{:S(2)}) copy-start(f32[128,128]{1,0:T(8,128)} %weight.3) | copy-start | bytes 196612
  63.5 1.3 collective-permute-start.3
  110.9 12.4 %copy-start.6 = (s32[128,4]{0,1:T(4,128)S(1)}, s32[128,4]{0,1:T(4,128)}, u32[]{:S(2)}) copy-start(s32[128,4]{0,1:T(4,128)} %param.11) | copy-start | bytes 6148
  116.1 1.3 collective-permute-start.4
  118.3 14.4 %all-to-all-start.10 = ((f32[64,1,128]{2,1,0:T(1,128)}), f32[64,1,128]{2,1,0:T(1,128)S(1)}, u32[]{:S(2)}, u32[]{:S(2)}) async-start(f32[64,1,128]{2,1,0:T(1,128)} %bitcast.13), calls=%async_computation.10 | async-start | bytes 65536 | tf_op jit(solution)/shard_map/all_to_all | solution.py:467
  132.7 4.0 %copy-start.5 = (s32[128,1]{0,1:T(1,128)S(1)}, s32[128,1]{0,1:T(1,128)}, u32[]{:S(2)}) copy-start(s32[128,1]{0,1:T(1,128)} %param.12) | copy-start | bytes 1540

commit v4 on v3

--- a/solution.py
+++ b/solution.py
@@ -12,7 +12,7 @@
 EPS = 1e-06
 ITERS = 2
 META = 8
-UNROLL = 32
+UNROLL = 64
 COPIES = 32
 EARLY = 8
 LIST = 640
@@ -366,7 +366,7 @@
     second = phi2 / rho2
     first = phi1 / rho1 - second * (theta1 / rho1)
     first, second = first / a0, second / a1
-    flag[...] = jnp.broadcast_to(alpha0[1:2, :], flag.shape)
+    flag[0, 0] = jnp.max(alpha0[1:2, :])
     n = sems.shape[0]
     each = out.shape[0] // n
 
@@ -390,8 +390,8 @@
 def general(blocks, col_index, row_counts, labels, row_weight, feature_scale):
     feat_local, side = feature_scale.shape
     peers = lax.axis_size("rows")
-    local_col = col_index - lax.axis_index("feat") * feat_local
-    live = (lax.broadcasted_iota(jnp.int32, col_index.shape, 1) < row_counts).astype(F32)
+    local_col = col_index.T - lax.axis_index("feat") * feat_local
+    live = (lax.broadcasted_iota(jnp.int32, local_col.shape, 0) < row_counts.T).astype(F32)
 
     def over_rows(x):
         return jnp.sum(lax.all_to_all(jnp.broadcast_to(x, (peers, 8, 128)), "rows", 0, 0), axis=0)[0, 0]
@@ -401,7 +401,7 @@
 
     def backward(resid):
         rowed = (row_weight * resid).astype(BF16)
-        terms = jnp.einsum("rsij,ri->rsj", blocks, rowed, preferred_element_type=F32) * live[:, :, None]
+        terms = jnp.einsum("rsij,ri->srj", blocks, rowed, preferred_element_type=F32) * live[:, :, None]
         partial = jax.ops.segment_sum(terms.reshape(-1, side), local_col.reshape(-1), num_segments=feat_local)
         owned = jnp.sum(lax.all_to_all(partial.reshape(peers, -1, side), "rows", 0, 0), axis=0)
         total = lax.all_to_all(jnp.broadcast_to(owned, (peers,) + owned.shape), "rows", 0, 0).reshape(feat_local, side)
@@ -421,8 +421,8 @@
         resid, beta, alpha, unit_feat, phi_bar, rho_bar, search, result = state
         scaled = (feature_scale * unit_feat).astype(BF16)
         picked = jnp.take(scaled, local_col, axis=0)
-        terms = jnp.einsum("rsij,rsj->rsi", blocks, picked, preferred_element_type=F32)
-        resid = row_weight * over_feat(jnp.sum(terms * live[:, :, None], axis=1)) - alpha * (resid / beta)
+        terms = jnp.einsum("rsij,srj->sri", blocks, picked, preferred_element_type=F32)
+        resid = row_weight * over_feat(jnp.sum(terms * live[:, :, None], axis=0)) - alpha * (resid / beta)
         total, beta = backward(resid)
         step_vec = feature_scale * total / beta - beta * unit_feat
         alpha = norm(step_vec)
@@ -550,10 +550,10 @@
     )(row_weight, mine, swap(mine), resid1, beta1)
     result, flag = pl.pallas_call(
         functools.partial(combine, own),
-        out_shape=(jax.ShapeDtypeStruct((feat_local, side), F32), small),
+        out_shape=(jax.ShapeDtypeStruct((feat_local, side), F32), jax.ShapeDtypeStruct((1, 1), F32)),
         in_specs=[vmem] * 8,
-        out_specs=(hbm, vmem),
-        scratch_shapes=[pltpu.VMEM((feat_local, side), F32), pltpu.SemaphoreType.DMA((16,))],
+        out_specs=(hbm, smem),
+        scratch_shapes=[pltpu.VMEM((feat_local, side), F32), pltpu.SemaphoreType.DMA((4,))],
         compiler_params=params,
         name="combine",
     )(recv0, recv1, feature_scale, exchange(send), beta0, alpha0, beta1, alpha1)
@@ -565,7 +565,7 @@
         args = (blocks, col_index, row_counts, labels, row_weight, feature_scale)
         return (jnp.zeros_like(state[0]),) + general(*lax.optimization_barrier((state[0],) + args)[1:])
 
-    _, result, resid2 = lax.while_loop(fits, again, (flag[0, 0], result, resid2))
+    _, result, resid2 = lax.while_loop(fits, again, (flag.reshape(()), result, resid2))
     return (result, resid2)
 
 

time: 138 us -> 135 us (0.978)
  blocking collectives: 88.8 us -> 103 us
  waiting for transfers between devices: 11.2 us -> 2.49 us
  starting transfers between devices: 5.14 us -> 0.17 us
  Pallas kernels: 29.6 us -> 26.9 us
    all_to_all x4 -> x5, blocking collectives: 88.8 us -> 103 us  [exchange(): return lax.all_to_all(x, 'rows', 0, 0)]
    all_to_all x1 -> x0, waiting for transfers between devices: 8.73 us -> none  [exchange(): return lax.all_to_all(x, 'rows', 0, 0)]
    all_to_all x1 -> x0, starting transfers between devices: 4.97 us -> none  [exchange(): return lax.all_to_all(x, 'rows', 0, 0)]
  transfers between devices with their start and end apart: 3 -> 2, of which waited for: 3 -> 2; matrix products, arithmetic and copies ran while one was open for 1% -> 0% of each run, Pallas kernels for 0% -> 0%
where the time goes in v4:
time: 135 us
  blocking collectives  103 us (76%)
  Pallas kernels  26.9 us (20%)
  waiting for transfers between devices  2.49 us (2%)
    all_to_all x5, blocking collectives, exchange(): return lax.all_to_all(x, 'rows', 0, 0)  103 us
    pallas_call x2, Pallas kernels, forward_part(): pl.pallas_call(functools.partial(forward, own), out_shape=part, in_specs=...  9.83 us
    pallas_call x1, Pallas kernels, body(): pl.pallas_call(functools.partial(first_backward, own), out_shape=(sparse,...  9.31 us
    pallas_call x1, Pallas kernels, body(): pl.pallas_call(next_backward, out_shape=(sparse, rowvec, small), in_specs...  3.85 us
  transfers between devices with their start and end apart: 2, of which 2 were waited for; matrix products, arithmetic and copies ran while one was open for 0% of the time, Pallas kernels for 0%

profile of v4, /device:TPU:0, one launch (start us, length us, event | category | flops | bytes accessed | tf_op | source)
XLA Modules:
  0.0 134.8 jit_solution(6494424497243593351)
XLA Ops:
  0.6 0.0 copy-start.1
  0.6 9.3 %backward0.1 = (bf16[64,32,128]{2,1,0:T(8,128)(2,1)S(1)}, bf16[512,128,128]{2,1,0:T(8,128)(2,1)S(1)}, s32[640]{0:T(1024)S(1)}, s32[640]{0:T(1024)S(1)}, f32[8,8,128]{2,1,0:T(8,128)S(1)}) custom-call(s32[4,128]{1,0:T(4,128)} %bitcast.99, s32[1,128]{1,0:T(1,128)} %bitcast.95, s32[128,128]{1,0:T(8,128)} %labels.1, f32[128,128]{1,0:T(8,128)} %weight.3, ...), custom_call_target="tpu_custom_call" | custom-call | tf_op jit(solution)/shard_map/backward0/pallas_call | solution.py:483
  10.0 24.6 %all_to_all.67.recv = bf16[64,32,128]{2,1,0:T(8,128)(2,1)S(1)} all-to-all(bf16[64,32,128]{2,1,0:T(8,128)(2,1)S(1)} %get-tuple-element.177), channel_id=1, replica_groups=mesh['rows'=64,'feat'=2] {'rows'}, dimensions={0} | all-to-all | bytes 1048576 | tf_op jit(solution)/shard_map/all_to_all | solution.py:467
  34.5 0.0 copy-done.1
  34.5 0.5 owner0.1
  35.0 23.2 %all_to_all.68.recv.recv0 = bf16[64,72,128]{2,1,0:T(8,128)(2,1)S(1)} all-to-all(bf16[64,72,128]{2,1,0:T(8,128)(2,1)S(1)} %get-tuple-element.178), channel_id=1, replica_groups=mesh['rows'=64,'feat'=2] {'rows'}, dimensions={0} | all-to-all | bytes 2359296 | tf_op jit(solution)/shard_map/all_to_all | solution.py:467
  58.2 0.0 copy-start.4
  58.2 0.0 copy-start.5
  58.2 4.9 %forward.2.mine = f32[136,128]{1,0:T(8,128)S(1)} custom-call(s32[640]{0:T(1024)S(1)} %get-tuple-element.180.codes, bf16[64,72,128]{2,1,0:T(8,128)(2,1)S(1)} %all_to_all.68.recv.recv0, f32[8,128]{1,0:T(8,128)S(1)} %get-tuple-element.181.scal.beta0, bf16[512,128,128]{2,1,0:T(8,128)(2,1)S(1)} %get-tuple-element.182.held), custom_call_target="tpu_custom_call" | custom-call | tf_op jit(solution)/shard_map/forward/pallas_call | solution.py:473
  63.2 0.1 collective-permute-start.3
  63.3 1.2 collective-permute-done.3.other
  64.5 0.0 copy-done.4
  64.5 0.0 copy-done.5
  64.5 3.8 %backward1.1 = (bf16[64,32,128]{2,1,0:T(8,128)(2,1)S(1)}, f32[128,128]{1,0:T(8,128)S(1)}, f32[8,128]{1,0:T(8,128)S(1)}) custom-call(s32[640]{0:T(1024)S(1)} %get-tuple-element.179.codes, s32[128,128]{1,0:T(8,128)S(1)} %copy-done.5, f32[128,128]{1,0:T(8,128)S(1)} %copy-done.4, f32[136,128]{1,0:T(8,128)S(1)} %forward.2.mine, ...), custom_call_target="tpu_custom_call" | custom-call | tf_op jit(solution)/shard_map/backward1/pallas_call | solution.py:523
  68.4 18.1 %all_to_all.69.recv = bf16[64,32,128]{2,1,0:T(8,128)(2,1)S(1)} all-to-all(bf16[64,32,128]{2,1,0:T(8,128)(2,1)S(1)} %get-tuple-element.184), channel_id=1, replica_groups=mesh['rows'=64,'feat'=2] {'rows'}, dimensions={0} | all-to-all | bytes 1048576 | tf_op jit(solution)/shard_map/all_to_all | solution.py:467
  86.5 0.5 owner1.1
  87.0 23.6 %all_to_all.70.recv.recv1 = bf16[64,72,128]{2,1,0:T(8,128)(2,1)S(1)} all-to-all(bf16[64,72,128]{2,1,0:T(8,128)(2,1)S(1)} %get-tuple-element.187), channel_id=1, replica_groups=mesh['rows'=64,'feat'=2] {'rows'}, dimensions={0} | all-to-all | bytes 2359296 | tf_op jit(solution)/shard_map/all_to_all | solution.py:467
  110.6 4.9 %forward.3.mine = f32[136,128]{1,0:T(8,128)S(1)} custom-call(s32[640]{0:T(1024)S(1)} %get-tuple-element.180.codes, bf16[64,72,128]{2,1,0:T(8,128)(2,1)S(1)} %all_to_all.70.recv.recv1, f32[8,128]{1,0:T(8,128)S(1)} %get-tuple-element.181.scal.beta0, bf16[512,128,128]{2,1,0:T(8,128)(2,1)S(1)} %get-tuple-element.182.held), custom_call_target="tpu_custom_call" | custom-call | tf_op jit(solution)/shard_map/forward/pallas_call | solution.py:473
  115.5 0.1 collective-permute-start.4
  115.6 1.2 collective-permute-done.4.other
  116.8 0.7 last_rows.1
  117.6 14.1 %all_to_all.71 = f32[64,1,128]{2,1,0:T(1,128)S(1)} all-to-all(f32[64,1,128]{2,1,0:T(1,128)S(1)} %bitcast.86), channel_id=1, replica_groups=mesh['rows'=64,'feat'=2] {'rows'}, dimensions={0} | all-to-all | bytes 65536 | tf_op jit(solution)/shard_map/all_to_all | solution.py:467
  131.6 0.0 copy-start.6
  131.6 0.0 copy-start.7
  131.6 2.1 %combine.1 = (f32[4096,128]{1,0:T(8,128)}, f32[1,1]{1,0:T(1,128)}) custom-call(bf16[64,72,128]{2,1,0:T(8,128)(2,1)S(1)} %all_to_all.68.recv.recv0, bf16[64,72,128]{2,1,0:T(8,128)(2,1)S(1)} %all_to_all.70.recv.recv1, f32[4096,128]{1,0:T(8,128)S(1)} %copy-done.1, f32[64,128]{1,0:T(8,128)S(1)} %bitcast.85, f32[8,128]{1,0:T(8,128)S(1)} %get-tuple-element.181.scal.beta0, ...), custom_call_target="tpu_custom_call" | custom-call | tf_op jit(solution)/shard_map/combine/pallas_call | solution.py:551
  133.8 0.0 copy-done.6
  133.8 0.0 copy-done.7
  133.8 0.8 while.36
Async XLA Ops:
  0.6 33.9 %copy-start.1 = (f32[4096,128]{1,0:T(8,128)S(1)}, f32[4096,128]{1,0:T(8,128)}, u32[]{:S(2)}) copy-start(f32[4096,128]{1,0:T(8,128)} %scale.1) | copy-start | bytes 6291460
  58.2 6.3 %copy-start.4 = (f32[128,128]{1,0:T(8,128)S(1)}, f32[128,128]{1,0:T(8,128)}, u32[]{:S(2)}) copy-start(f32[128,128]{1,0:T(8,128)} %weight.3) | copy-start | bytes 196612
  58.2 6.3 %copy-start.5 = (s32[128,128]{1,0:T(8,128)S(1)}, s32[128,128]{1,0:T(8,128)}, u32[]{:S(2)}) copy-start(s32[128,128]{1,0:T(8,128)} %labels.1) | copy-start | bytes 196612
  63.2 1.3 collective-permute-start.3
  115.5 1.3 collective-permute-start.4
  131.6 2.1 %copy-start.6 = (s32[128,1]{0,1:T(1,128)S(1)}, s32[128,1]{0,1:T(1,128)}, u32[]{:S(2)}) copy-start(s32[128,1]{0,1:T(1,128)} %param.12) | copy-start | bytes 1540
  131.6 2.2 %copy-start.7 = (s32[128,4]{0,1:T(4,128)S(1)}, s32[128,4]{0,1:T(4,128)}, u32[]{:S(2)}) copy-start(s32[128,4]{0,1:T(4,128)} %param.11) | copy-start | bytes 6148

commit v5 on v4

--- a/solution.py
+++ b/solution.py
@@ -13,8 +13,8 @@
 ITERS = 2
 META = 8
 UNROLL = 64
-COPIES = 32
-EARLY = 8
+COPIES = 16
+EARLY = 1
 LIST = 640
 TABLES = 4
 PACKET = 32
@@ -154,7 +154,7 @@
     return weight[...] * (2 * labels[...] - 1).astype(F32)
 
 
-def place_entries(own, peers, cols, counts, places, index):
+def place_entries(own, peers, cols, counts, entries, index):
     slots, rows = cols.shape
     first = lax.axis_index("feat") * (own * peers)
     lane0 = (lax.axis_index("rows") & 3) * PACKET
@@ -172,7 +172,11 @@
         before = before + jnp.sum(hit, axis=1, keepdims=True)
         rank = jnp.sum(hit * rank, axis=0, keepdims=True).astype(jnp.int32)
         fits = live & (rank < ROOM)
-        places[s : s + 1, :] = jnp.where(fits, owner * PACKET + rank, peers * PACKET)
+        across = lax.broadcasted_iota(jnp.int32, (1, rows), 1)
+        code = (across << 12) | ((across * slots + s) << 20)
+        entries[s : s + 1, :] = code | jnp.where(fits, owner * PACKET + rank, peers * PACKET)
+        entries[slots + s : slots + s + 1, :] = code | c
+        entries[2 * slots + s : 2 * slots + s + 1, :] = jnp.where(live, 1, 0)
         lane = jnp.where(fits, rank + lane0, -1)
         known = ((c & (own - 1)) + 1).astype(F32)
         spot = jnp.where(down == lane, 1.0, 0.0).astype(BF16)
@@ -185,28 +189,26 @@
 
 def first_backward(
     own, col_hbm, cnt_hbm, labels_hbm, weight_hbm, blocks, out, held, forth, back, index,
-    cols, counts, col, cnt, places, labels, weight, wide, place_tile, stage, meta, sems, small_sems,
+    cols, counts, entries, labels, weight, wide, entry_tile, stage, meta, sems, small_sems,
 ):
     slots, rows = cols.shape
     each = held.shape[0] // COPIES
     per_step = 8 * slots // each
-    first = lax.axis_index("feat") * (own * out.shape[0])
 
     def block_copy(i):
         at = pl.ds(i * each, each)
         return pltpu.make_async_copy(blocks.at[at], held.at[at], sems.at[i])
 
-    pairs = ((col_hbm, cols), (cnt_hbm, counts), (labels_hbm, labels), (weight_hbm, weight), (col_hbm, col), (cnt_hbm, cnt))
+    pairs = ((col_hbm, cols), (cnt_hbm, counts), (labels_hbm, labels), (weight_hbm, weight))
     small = [pltpu.make_async_copy(src, dst, small_sems.at[i]) for i, (src, dst) in enumerate(pairs)]
     for copy in small:
         copy.start()
     for i in range(EARLY):
         block_copy(i).start()
-    clear(stage)
     for copy in small:
         copy.wait()
-    flag = place_entries(own, out.shape[0], cols, counts, place_tile, index)
-    to_scalars = pltpu.make_async_copy(place_tile, places, small_sems.at[len(pairs)])
+    flag = place_entries(own, out.shape[0], cols, counts, entry_tile, index)
+    to_scalars = pltpu.make_async_copy(entry_tile, entries, small_sems.at[len(pairs)])
     to_scalars.start(priority=1)
     for i in range(EARLY, COPIES):
         block_copy(i).start()
@@ -215,6 +217,7 @@
     odd = lax.broadcasted_iota(jnp.int32, rowed.shape, 0) & 1
     wide[:, 0:128] = jnp.where(odd == 0, rowed, 0.0)
     wide[:, 128:256] = jnp.where(odd == 1, rowed, 0.0)
+    clear(stage)
     to_scalars.wait()
 
     def step(p, k):
@@ -229,12 +232,11 @@
                 for u in range(4):
                     m, slot = 2 * pair + u // 2, 2 * h + u % 2
                     r = r0 + m
-                    place = places[slot, r]
-                    put_row(stage, place, pick(t, m, u % 2, False))
-                    code = (r << 12) | (e[u] << 20)
-                    forth[k] = code | (col[slot, r] - first)
-                    back[k] = code | place
-                    k = k + (slot < cnt[0, r]).astype(jnp.int32)
+                    code = entries[slot, r]
+                    put_row(stage, code & 4095, pick(t, m, u % 2, False))
+                    back[k] = code
+                    forth[k] = entries[slots + slot, r]
+                    k = k + entries[2 * slots + slot, r]
         return k
 
     live = lax.fori_loop(0, rows // 8, step, 0)
@@ -494,17 +496,15 @@
         scratch_shapes=[
             pltpu.VMEM((slots, rows), jnp.int32),
             pltpu.VMEM((1, rows), jnp.int32),
-            pltpu.SMEM((slots, rows), jnp.int32),
-            pltpu.SMEM((1, rows), jnp.int32),
-            pltpu.SMEM((slots, rows), jnp.int32),
+            pltpu.SMEM((3 * slots, rows), jnp.int32),
             pltpu.VMEM((rows, side), jnp.int32),
             pltpu.VMEM((rows, side), F32),
             pltpu.VMEM((rows, 2 * side), F32),
-            pltpu.VMEM((slots, rows), jnp.int32),
+            pltpu.VMEM((3 * slots, rows), jnp.int32),
             stage,
             mark,
             pltpu.SemaphoreType.DMA((COPIES,)),
-            pltpu.SemaphoreType.DMA((7,)),
+            pltpu.SemaphoreType.DMA((5,)),
         ],
         compiler_params=params,
         name="backward0",

time: 135 us -> 133 us (0.985)
  Pallas kernels: 26.9 us -> 23.9 us
  blocking collectives: 103 us -> 105 us
    all_to_all x5, blocking collectives: 103 us -> 105 us  [exchange(): return lax.all_to_all(x, 'rows', 0, 0)]
where the time goes in v5:
time: 133 us
  blocking collectives  105 us (79%)
  Pallas kernels  23.9 us (18%)
  waiting for transfers between devices  2.49 us (2%)
    all_to_all x5, blocking collectives, exchange(): return lax.all_to_all(x, 'rows', 0, 0)  105 us
    pallas_call x2, Pallas kernels, forward_part(): pl.pallas_call(functools.partial(forward, own), out_shape=part, in_specs=...  8.5 us
    pallas_call x1, Pallas kernels, body(): pl.pallas_call(functools.partial(first_backward, own), out_shape=(sparse,...  8.06 us
    pallas_call x1, Pallas kernels, body(): pl.pallas_call(next_backward, out_shape=(sparse, rowvec, small), in_specs...  3.4 us
  transfers between devices with their start and end apart: 2, of which 2 were waited for; matrix products, arithmetic and copies ran while one was open for 0% of the time, Pallas kernels for 0%

profile of v5, /device:TPU:0, one launch (start us, length us, event | category | flops | bytes accessed | tf_op | source)
XLA Modules:
  0.0 133.2 jit_solution(7807887207423557505)
XLA Ops:
  0.6 0.0 copy-start.1
  0.6 8.1 %backward0.1 = (bf16[64,32,128]{2,1,0:T(8,128)(2,1)S(1)}, bf16[512,128,128]{2,1,0:T(8,128)(2,1)S(1)}, s32[640]{0:T(1024)S(1)}, s32[640]{0:T(1024)S(1)}, f32[8,8,128]{2,1,0:T(8,128)S(1)}) custom-call(s32[4,128]{1,0:T(4,128)} %bitcast.99, s32[1,128]{1,0:T(1,128)} %bitcast.95, s32[128,128]{1,0:T(8,128)} %labels.1, f32[128,128]{1,0:T(8,128)} %weight.3, ...), custom_call_target="tpu_custom_call" | custom-call | tf_op jit(solution)/shard_map/backward0/pallas_call | solution.py:485
  8.7 24.6 %all_to_all.67.recv = bf16[64,32,128]{2,1,0:T(8,128)(2,1)S(1)} all-to-all(bf16[64,32,128]{2,1,0:T(8,128)(2,1)S(1)} %get-tuple-element.177), channel_id=1, replica_groups=mesh['rows'=64,'feat'=2] {'rows'}, dimensions={0} | all-to-all | bytes 1048576 | tf_op jit(solution)/shard_map/all_to_all | solution.py:469
  33.3 0.0 copy-done.1
  33.3 0.5 owner0.1
  33.8 23.2 %all_to_all.68.recv.recv0 = bf16[64,72,128]{2,1,0:T(8,128)(2,1)S(1)} all-to-all(bf16[64,72,128]{2,1,0:T(8,128)(2,1)S(1)} %get-tuple-element.178), channel_id=1, replica_groups=mesh['rows'=64,'feat'=2] {'rows'}, dimensions={0} | all-to-all | bytes 2359296 | tf_op jit(solution)/shard_map/all_to_all | solution.py:469
  57.0 0.0 copy-start.4
  57.0 0.0 copy-start.5
  57.0 4.2 %forward.2.mine = f32[136,128]{1,0:T(8,128)S(1)} custom-call(s32[640]{0:T(1024)S(1)} %get-tuple-element.180.codes, bf16[64,72,128]{2,1,0:T(8,128)(2,1)S(1)} %all_to_all.68.recv.recv0, f32[8,128]{1,0:T(8,128)S(1)} %get-tuple-element.181.scal.beta0, bf16[512,128,128]{2,1,0:T(8,128)(2,1)S(1)} %get-tuple-element.182.held), custom_call_target="tpu_custom_call" | custom-call | tf_op jit(solution)/shard_map/forward/pallas_call | solution.py:475
  61.2 0.1 collective-permute-start.3
  61.3 1.2 collective-permute-done.3.other
  62.6 0.0 copy-done.4
  62.6 0.0 copy-done.5
  62.6 3.4 %backward1.1 = (bf16[64,32,128]{2,1,0:T(8,128)(2,1)S(1)}, f32[128,128]{1,0:T(8,128)S(1)}, f32[8,128]{1,0:T(8,128)S(1)}) custom-call(s32[640]{0:T(1024)S(1)} %get-tuple-element.179.codes, s32[128,128]{1,0:T(8,128)S(1)} %copy-done.5, f32[128,128]{1,0:T(8,128)S(1)} %copy-done.4, f32[136,128]{1,0:T(8,128)S(1)} %forward.2.mine, ...), custom_call_target="tpu_custom_call" | custom-call | tf_op jit(solution)/shard_map/backward1/pallas_call | solution.py:523
  66.0 19.1 %all_to_all.69.recv = bf16[64,32,128]{2,1,0:T(8,128)(2,1)S(1)} all-to-all(bf16[64,32,128]{2,1,0:T(8,128)(2,1)S(1)} %get-tuple-element.184), channel_id=1, replica_groups=mesh['rows'=64,'feat'=2] {'rows'}, dimensions={0} | all-to-all | bytes 1048576 | tf_op jit(solution)/shard_map/all_to_all | solution.py:469
  85.1 0.5 owner1.1
  85.6 23.4 %all_to_all.70.recv.recv1 = bf16[64,72,128]{2,1,0:T(8,128)(2,1)S(1)} all-to-all(bf16[64,72,128]{2,1,0:T(8,128)(2,1)S(1)} %get-tuple-element.187), channel_id=1, replica_groups=mesh['rows'=64,'feat'=2] {'rows'}, dimensions={0} | all-to-all | bytes 2359296 | tf_op jit(solution)/shard_map/all_to_all | solution.py:469
  109.0 4.2 %forward.3.mine = f32[136,128]{1,0:T(8,128)S(1)} custom-call(s32[640]{0:T(1024)S(1)} %get-tuple-element.180.codes, bf16[64,72,128]{2,1,0:T(8,128)(2,1)S(1)} %all_to_all.70.recv.recv1, f32[8,128]{1,0:T(8,128)S(1)} %get-tuple-element.181.scal.beta0, bf16[512,128,128]{2,1,0:T(8,128)(2,1)S(1)} %get-tuple-element.182.held), custom_call_target="tpu_custom_call" | custom-call | tf_op jit(solution)/shard_map/forward/pallas_call | solution.py:475
  113.3 0.1 collective-permute-start.4
  113.3 1.2 collective-permute-done.4.other
  114.6 0.7 last_rows.1
  115.3 14.7 %all_to_all.71 = f32[64,1,128]{2,1,0:T(1,128)S(1)} all-to-all(f32[64,1,128]{2,1,0:T(1,128)S(1)} %bitcast.86), channel_id=1, replica_groups=mesh['rows'=64,'feat'=2] {'rows'}, dimensions={0} | all-to-all | bytes 65536 | tf_op jit(solution)/shard_map/all_to_all | solution.py:469
  130.1 0.0 copy-start.6
  130.1 0.0 copy-start.7
  130.1 2.1 %combine.1 = (f32[4096,128]{1,0:T(8,128)}, f32[1,1]{1,0:T(1,128)}) custom-call(bf16[64,72,128]{2,1,0:T(8,128)(2,1)S(1)} %all_to_all.68.recv.recv0, bf16[64,72,128]{2,1,0:T(8,128)(2,1)S(1)} %all_to_all.70.recv.recv1, f32[4096,128]{1,0:T(8,128)S(1)} %copy-done.1, f32[64,128]{1,0:T(8,128)S(1)} %bitcast.85, f32[8,128]{1,0:T(8,128)S(1)} %get-tuple-element.181.scal.beta0, ...), custom_call_target="tpu_custom_call" | custom-call | tf_op jit(solution)/shard_map/combine/pallas_call | solution.py:551
  132.2 0.0 copy-done.6
  132.2 0.0 copy-done.7
  132.2 0.8 while.36
Async XLA Ops:
  0.6 32.7 %copy-start.1 = (f32[4096,128]{1,0:T(8,128)S(1)}, f32[4096,128]{1,0:T(8,128)}, u32[]{:S(2)}) copy-start(f32[4096,128]{1,0:T(8,128)} %scale.1) | copy-start | bytes 6291460
  57.0 5.6 %copy-start.4 = (f32[128,128]{1,0:T(8,128)S(1)}, f32[128,128]{1,0:T(8,128)}, u32[]{:S(2)}) copy-start(f32[128,128]{1,0:T(8,128)} %weight.3) | copy-start | bytes 196612
  57.0 5.6 %copy-start.5 = (s32[128,128]{1,0:T(8,128)S(1)}, s32[128,128]{1,0:T(8,128)}, u32[]{:S(2)}) copy-start(s32[128,128]{1,0:T(8,128)} %labels.1) | copy-start | bytes 196612
  61.2 1.3 %collective-permute-start.3 = (f32[136,128]{1,0:T(8,128)S(1)}, f32[136,128]{1,0:T(8,128)S(1)}, u32[]{:S(2)}, u32[]{:S(2)}) collective-permute-start(f32[136,128]{1,0:T(8,128)S(1)} %forward.2.mine), channel_id=1, source_target_pairs={{0,1},{1,0},{2,3},{3,2},{4,5},{5,4},{6,7},{7,6},{8,9},{9,8},{10,11... | collective-permute-start | bytes 208904 | tf_op jit(solution)/shard_map/ppermute | solution.py:472
  113.3 1.3 %collective-permute-start.4 = (f32[136,128]{1,0:T(8,128)S(1)}, f32[136,128]{1,0:T(8,128)S(1)}, u32[]{:S(2)}, u32[]{:S(2)}) collective-permute-start(f32[136,128]{1,0:T(8,128)S(1)} %forward.3.mine), channel_id=1, source_target_pairs={{0,1},{1,0},{2,3},{3,2},{4,5},{5,4},{6,7},{7,6},{8,9},{9,8},{10,11... | collective-permute-start | bytes 208904 | tf_op jit(solution)/shard_map/ppermute | solution.py:472
  130.1 2.1 %copy-start.6 = (s32[128,1]{0,1:T(1,128)S(1)}, s32[128,1]{0,1:T(1,128)}, u32[]{:S(2)}) copy-start(s32[128,1]{0,1:T(1,128)} %param.12) | copy-start | bytes 1540
  130.1 2.2 %copy-start.7 = (s32[128,4]{0,1:T(4,128)S(1)}, s32[128,4]{0,1:T(4,128)}, u32[]{:S(2)}) copy-start(s32[128,4]{0,1:T(4,128)} %param.11) | copy-start | bytes 6148

commit v6 on v5

--- a/solution.py
+++ b/solution.py
@@ -205,13 +205,15 @@
         copy.start()
     for i in range(EARLY):
         block_copy(i).start()
-    for copy in small:
+    for copy in small[:2]:
         copy.wait()
     flag = place_entries(own, out.shape[0], cols, counts, entry_tile, index)
     to_scalars = pltpu.make_async_copy(entry_tile, entries, small_sems.at[len(pairs)])
     to_scalars.start(priority=1)
     for i in range(EARLY, COPIES):
         block_copy(i).start()
+    for copy in small[2:]:
+        copy.wait()
     resid = rhs_of(labels, weight)
     rowed = (weight[...] * resid).astype(BF16).astype(F32)
     odd = lax.broadcasted_iota(jnp.int32, rowed.shape, 0) & 1
@@ -332,7 +334,7 @@
         table[pl.ds(d * tiles, tiles)] = recv[d, 0:own, :].astype(F32).reshape(tiles, 8, 128)
         return meta + recv[d, own : own + META, :].astype(F32)
 
-    meta = lax.fori_loop(0, recv.shape[0], fill, jnp.zeros((META, 128), F32), unroll=2)
+    meta = lax.fori_loop(0, recv.shape[0], fill, jnp.zeros((META, 128), F32), unroll=8)
     row = lax.broadcasted_iota(jnp.int32, (META, 128), 0)
     out[rows:, :] = jnp.where(row == 3, scal[1:2, :], meta)
     for ref in outs:

time: 133 us -> 133 us (level)
  blocking collectives: 105 us -> 103 us
  Pallas kernels: 23.9 us -> 25.3 us
    all_to_all x5, blocking collectives: 105 us -> 103 us  [exchange(): return lax.all_to_all(x, 'rows', 0, 0)]
where the time goes in v6:
time: 133 us
  blocking collectives  103 us (77%)
  Pallas kernels  25.3 us (19%)
  waiting for transfers between devices  2.49 us (2%)
    all_to_all x5, blocking collectives, exchange(): return lax.all_to_all(x, 'rows', 0, 0)  103 us
    pallas_call x2, Pallas kernels, forward_part(): pl.pallas_call(functools.partial(forward, own), out_shape=part, in_specs=...  9.67 us
    pallas_call x1, Pallas kernels, body(): pl.pallas_call(functools.partial(first_backward, own), out_shape=(sparse,...  7.87 us
    pallas_call x1, Pallas kernels, body(): pl.pallas_call(next_backward, out_shape=(sparse, rowvec, small), in_specs...  3.85 us
  transfers between devices with their start and end apart: 2, of which 2 were waited for; matrix products, arithmetic and copies ran while one was open for 0% of the time, Pallas kernels for 0%

profile of v6, /device:TPU:0, one launch (start us, length us, event | category | flops | bytes accessed | tf_op | source)
XLA Modules:
  0.0 132.9 jit_solution(3959511857686532214)
XLA Ops:
  0.6 0.0 copy-start.1
  0.6 7.9 %backward0.1 = (bf16[64,32,128]{2,1,0:T(8,128)(2,1)S(1)}, bf16[512,128,128]{2,1,0:T(8,128)(2,1)S(1)}, s32[640]{0:T(1024)S(1)}, s32[640]{0:T(1024)S(1)}, f32[8,8,128]{2,1,0:T(8,128)S(1)}) custom-call(s32[4,128]{1,0:T(4,128)} %bitcast.99, s32[1,128]{1,0:T(1,128)} %bitcast.95, s32[128,128]{1,0:T(8,128)} %labels.1, f32[128,128]{1,0:T(8,128)} %weight.3, ...), custom_call_target="tpu_custom_call" | custom-call | tf_op jit(solution)/shard_map/backward0/pallas_call | solution.py:487
  8.5 24.6 %all_to_all.67.recv = bf16[64,32,128]{2,1,0:T(8,128)(2,1)S(1)} all-to-all(bf16[64,32,128]{2,1,0:T(8,128)(2,1)S(1)} %get-tuple-element.177), channel_id=1, replica_groups=mesh['rows'=64,'feat'=2] {'rows'}, dimensions={0} | all-to-all | bytes 1048576 | tf_op jit(solution)/shard_map/all_to_all | solution.py:471
  33.1 0.0 copy-done.1
  33.1 0.5 owner0.1
  33.6 23.2 %all_to_all.68.recv.recv0 = bf16[64,72,128]{2,1,0:T(8,128)(2,1)S(1)} all-to-all(bf16[64,72,128]{2,1,0:T(8,128)(2,1)S(1)} %get-tuple-element.178), channel_id=1, replica_groups=mesh['rows'=64,'feat'=2] {'rows'}, dimensions={0} | all-to-all | bytes 2359296 | tf_op jit(solution)/shard_map/all_to_all | solution.py:471
  56.8 0.0 copy-start.4
  56.8 0.0 copy-start.5
  56.8 4.8 %forward.2.mine = f32[136,128]{1,0:T(8,128)S(1)} custom-call(s32[640]{0:T(1024)S(1)} %get-tuple-element.180.codes, bf16[64,72,128]{2,1,0:T(8,128)(2,1)S(1)} %all_to_all.68.recv.recv0, f32[8,128]{1,0:T(8,128)S(1)} %get-tuple-element.181.scal.beta0, bf16[512,128,128]{2,1,0:T(8,128)(2,1)S(1)} %get-tuple-element.182.held), custom_call_target="tpu_custom_call" | custom-call | tf_op jit(solution)/shard_map/forward/pallas_call | solution.py:477
  61.6 0.1 collective-permute-start.3
  61.7 1.2 collective-permute-done.3.other
  63.0 0.0 copy-done.4
  63.0 0.0 copy-done.5
  63.0 3.8 %backward1.1 = (bf16[64,32,128]{2,1,0:T(8,128)(2,1)S(1)}, f32[128,128]{1,0:T(8,128)S(1)}, f32[8,128]{1,0:T(8,128)S(1)}) custom-call(s32[640]{0:T(1024)S(1)} %get-tuple-element.179.codes, s32[128,128]{1,0:T(8,128)S(1)} %copy-done.5, f32[128,128]{1,0:T(8,128)S(1)} %copy-done.4, f32[136,128]{1,0:T(8,128)S(1)} %forward.2.mine, ...), custom_call_target="tpu_custom_call" | custom-call | tf_op jit(solution)/shard_map/backward1/pallas_call | solution.py:525
  66.8 17.9 %all_to_all.69.recv = bf16[64,32,128]{2,1,0:T(8,128)(2,1)S(1)} all-to-all(bf16[64,32,128]{2,1,0:T(8,128)(2,1)S(1)} %get-tuple-element.184), channel_id=1, replica_groups=mesh['rows'=64,'feat'=2] {'rows'}, dimensions={0} | all-to-all | bytes 1048576 | tf_op jit(solution)/shard_map/all_to_all | solution.py:471
  84.8 0.5 owner1.1
  85.3 23.6 %all_to_all.70.recv.recv1 = bf16[64,72,128]{2,1,0:T(8,128)(2,1)S(1)} all-to-all(bf16[64,72,128]{2,1,0:T(8,128)(2,1)S(1)} %get-tuple-element.187), channel_id=1, replica_groups=mesh['rows'=64,'feat'=2] {'rows'}, dimensions={0} | all-to-all | bytes 2359296 | tf_op jit(solution)/shard_map/all_to_all | solution.py:471
  108.9 4.8 %forward.3.mine = f32[136,128]{1,0:T(8,128)S(1)} custom-call(s32[640]{0:T(1024)S(1)} %get-tuple-element.180.codes, bf16[64,72,128]{2,1,0:T(8,128)(2,1)S(1)} %all_to_all.70.recv.recv1, f32[8,128]{1,0:T(8,128)S(1)} %get-tuple-element.181.scal.beta0, bf16[512,128,128]{2,1,0:T(8,128)(2,1)S(1)} %get-tuple-element.182.held), custom_call_target="tpu_custom_call" | custom-call | tf_op jit(solution)/shard_map/forward/pallas_call | solution.py:477
  113.7 0.1 collective-permute-start.4
  113.8 1.2 collective-permute-done.4.other
  115.1 0.7 last_rows.1
  115.8 13.9 %all_to_all.71 = f32[64,1,128]{2,1,0:T(1,128)S(1)} all-to-all(f32[64,1,128]{2,1,0:T(1,128)S(1)} %bitcast.86), channel_id=1, replica_groups=mesh['rows'=64,'feat'=2] {'rows'}, dimensions={0} | all-to-all | bytes 65536 | tf_op jit(solution)/shard_map/all_to_all | solution.py:471
  129.7 0.0 copy-start.6
  129.7 0.0 copy-start.7
  129.7 2.1 %combine.1 = (f32[4096,128]{1,0:T(8,128)}, f32[1,1]{1,0:T(1,128)}) custom-call(bf16[64,72,128]{2,1,0:T(8,128)(2,1)S(1)} %all_to_all.68.recv.recv0, bf16[64,72,128]{2,1,0:T(8,128)(2,1)S(1)} %all_to_all.70.recv.recv1, f32[4096,128]{1,0:T(8,128)S(1)} %copy-done.1, f32[64,128]{1,0:T(8,128)S(1)} %bitcast.85, f32[8,128]{1,0:T(8,128)S(1)} %get-tuple-element.181.scal.beta0, ...), custom_call_target="tpu_custom_call" | custom-call | tf_op jit(solution)/shard_map/combine/pallas_call | solution.py:553
  131.8 0.0 copy-done.6
  131.8 0.0 copy-done.7
  131.8 0.8 while.36
Async XLA Ops:
  0.6 32.5 %copy-start.1 = (f32[4096,128]{1,0:T(8,128)S(1)}, f32[4096,128]{1,0:T(8,128)}, u32[]{:S(2)}) copy-start(f32[4096,128]{1,0:T(8,128)} %scale.1) | copy-start | bytes 6291460
  56.8 6.2 %copy-start.4 = (f32[128,128]{1,0:T(8,128)S(1)}, f32[128,128]{1,0:T(8,128)}, u32[]{:S(2)}) copy-start(f32[128,128]{1,0:T(8,128)} %weight.3) | copy-start | bytes 196612
  56.8 6.2 %copy-start.5 = (s32[128,128]{1,0:T(8,128)S(1)}, s32[128,128]{1,0:T(8,128)}, u32[]{:S(2)}) copy-start(s32[128,128]{1,0:T(8,128)} %labels.1) | copy-start | bytes 196612
  61.6 1.3 %collective-permute-start.3 = (f32[136,128]{1,0:T(8,128)S(1)}, f32[136,128]{1,0:T(8,128)S(1)}, u32[]{:S(2)}, u32[]{:S(2)}) collective-permute-start(f32[136,128]{1,0:T(8,128)S(1)} %forward.2.mine), channel_id=1, source_target_pairs={{0,1},{1,0},{2,3},{3,2},{4,5},{5,4},{6,7},{7,6},{8,9},{9,8},{10,11... | collective-permute-start | bytes 208904 | tf_op jit(solution)/shard_map/ppermute | solution.py:474
  113.7 1.3 %collective-permute-start.4 = (f32[136,128]{1,0:T(8,128)S(1)}, f32[136,128]{1,0:T(8,128)S(1)}, u32[]{:S(2)}, u32[]{:S(2)}) collective-permute-start(f32[136,128]{1,0:T(8,128)S(1)} %forward.3.mine), channel_id=1, source_target_pairs={{0,1},{1,0},{2,3},{3,2},{4,5},{5,4},{6,7},{7,6},{8,9},{9,8},{10,11... | collective-permute-start | bytes 208904 | tf_op jit(solution)/shard_map/ppermute | solution.py:474
  129.7 2.1 %copy-start.6 = (s32[128,1]{0,1:T(1,128)S(1)}, s32[128,1]{0,1:T(1,128)}, u32[]{:S(2)}) copy-start(s32[128,1]{0,1:T(1,128)} %param.12) | copy-start | bytes 1540
  129.7 2.2 %copy-start.7 = (s32[128,4]{0,1:T(4,128)S(1)}, s32[128,4]{0,1:T(4,128)}, u32[]{:S(2)}) copy-start(s32[128,4]{0,1:T(4,128)} %param.11) | copy-start | bytes 6148

commit v7 on v6

--- a/solution.py
+++ b/solution.py
@@ -12,7 +12,7 @@
 EPS = 1e-06
 ITERS = 2
 META = 8
-UNROLL = 64
+UNROLL = 72
 COPIES = 16
 EARLY = 1
 LIST = 640

time: 133 us -> 133 us (level)
  no operation moved by 1% of the time
where the time goes in v7:
time: 133 us; the launch traced here: 132 us
  blocking collectives  103 us (77%)
  Pallas kernels  24.4 us (18%)
  waiting for transfers between devices  2.49 us (2%)
    all_to_all x5, blocking collectives, exchange(): return lax.all_to_all(x, 'rows', 0, 0)  103 us
    pallas_call x2, Pallas kernels, forward_part(): pl.pallas_call(functools.partial(forward, own), out_shape=part, in_specs=...  9 us
    pallas_call x1, Pallas kernels, body(): pl.pallas_call(functools.partial(first_backward, own), out_shape=(sparse,...  7.87 us
    pallas_call x1, Pallas kernels, body(): pl.pallas_call(next_backward, out_shape=(sparse, rowvec, small), in_specs...  3.64 us
  transfers between devices with their start and end apart: 2, of which 2 were waited for; matrix products, arithmetic and copies ran while one was open for 0% of the time, Pallas kernels for 0%

profile of v7, /device:TPU:0, one launch (start us, length us, event | category | flops | bytes accessed | tf_op | source)
XLA Modules:
  0.0 132.3 jit_solution(15171199423908703275)
XLA Ops:
  0.6 0.0 copy-start.1
  0.6 7.9 %backward0.1 = (bf16[64,32,128]{2,1,0:T(8,128)(2,1)S(1)}, bf16[512,128,128]{2,1,0:T(8,128)(2,1)S(1)}, s32[640]{0:T(1024)S(1)}, s32[640]{0:T(1024)S(1)}, f32[8,8,128]{2,1,0:T(8,128)S(1)}) custom-call(s32[4,128]{1,0:T(4,128)} %bitcast.99, s32[1,128]{1,0:T(1,128)} %bitcast.95, s32[128,128]{1,0:T(8,128)} %labels.1, f32[128,128]{1,0:T(8,128)} %weight.3, ...), custom_call_target="tpu_custom_call" | custom-call | tf_op jit(solution)/shard_map/backward0/pallas_call | solution.py:487
  8.5 24.6 %all_to_all.67.recv = bf16[64,32,128]{2,1,0:T(8,128)(2,1)S(1)} all-to-all(bf16[64,32,128]{2,1,0:T(8,128)(2,1)S(1)} %get-tuple-element.177), channel_id=1, replica_groups=mesh['rows'=64,'feat'=2] {'rows'}, dimensions={0} | all-to-all | bytes 1048576 | tf_op jit(solution)/shard_map/all_to_all | solution.py:471
  33.1 0.0 copy-done.1
  33.1 0.5 owner0.1
  33.6 23.2 %all_to_all.68.recv.recv0 = bf16[64,72,128]{2,1,0:T(8,128)(2,1)S(1)} all-to-all(bf16[64,72,128]{2,1,0:T(8,128)(2,1)S(1)} %get-tuple-element.178), channel_id=1, replica_groups=mesh['rows'=64,'feat'=2] {'rows'}, dimensions={0} | all-to-all | bytes 2359296 | tf_op jit(solution)/shard_map/all_to_all | solution.py:471
  56.8 0.0 copy-start.4
  56.8 0.0 copy-start.5
  56.8 4.5 %forward.2.mine = f32[136,128]{1,0:T(8,128)S(1)} custom-call(s32[640]{0:T(1024)S(1)} %get-tuple-element.180.codes, bf16[64,72,128]{2,1,0:T(8,128)(2,1)S(1)} %all_to_all.68.recv.recv0, f32[8,128]{1,0:T(8,128)S(1)} %get-tuple-element.181.scal.beta0, bf16[512,128,128]{2,1,0:T(8,128)(2,1)S(1)} %get-tuple-element.182.held), custom_call_target="tpu_custom_call" | custom-call | tf_op jit(solution)/shard_map/forward/pallas_call | solution.py:477
  61.3 0.1 collective-permute-start.3
  61.4 1.2 collective-permute-done.3.other
  62.6 0.0 copy-done.4
  62.6 0.0 copy-done.5
  62.6 3.6 %backward1.1 = (bf16[64,32,128]{2,1,0:T(8,128)(2,1)S(1)}, f32[128,128]{1,0:T(8,128)S(1)}, f32[8,128]{1,0:T(8,128)S(1)}) custom-call(s32[640]{0:T(1024)S(1)} %get-tuple-element.179.codes, s32[128,128]{1,0:T(8,128)S(1)} %copy-done.5, f32[128,128]{1,0:T(8,128)S(1)} %copy-done.4, f32[136,128]{1,0:T(8,128)S(1)} %forward.2.mine, ...), custom_call_target="tpu_custom_call" | custom-call | tf_op jit(solution)/shard_map/backward1/pallas_call | solution.py:525
  66.3 18.1 %all_to_all.69.recv = bf16[64,32,128]{2,1,0:T(8,128)(2,1)S(1)} all-to-all(bf16[64,32,128]{2,1,0:T(8,128)(2,1)S(1)} %get-tuple-element.184), channel_id=1, replica_groups=mesh['rows'=64,'feat'=2] {'rows'}, dimensions={0} | all-to-all | bytes 1048576 | tf_op jit(solution)/shard_map/all_to_all | solution.py:471
  84.4 0.5 owner1.1
  85.0 23.5 %all_to_all.70.recv.recv1 = bf16[64,72,128]{2,1,0:T(8,128)(2,1)S(1)} all-to-all(bf16[64,72,128]{2,1,0:T(8,128)(2,1)S(1)} %get-tuple-element.187), channel_id=1, replica_groups=mesh['rows'=64,'feat'=2] {'rows'}, dimensions={0} | all-to-all | bytes 2359296 | tf_op jit(solution)/shard_map/all_to_all | solution.py:471
  108.5 4.5 %forward.3.mine = f32[136,128]{1,0:T(8,128)S(1)} custom-call(s32[640]{0:T(1024)S(1)} %get-tuple-element.180.codes, bf16[64,72,128]{2,1,0:T(8,128)(2,1)S(1)} %all_to_all.70.recv.recv1, f32[8,128]{1,0:T(8,128)S(1)} %get-tuple-element.181.scal.beta0, bf16[512,128,128]{2,1,0:T(8,128)(2,1)S(1)} %get-tuple-element.182.held), custom_call_target="tpu_custom_call" | custom-call | tf_op jit(solution)/shard_map/forward/pallas_call | solution.py:477
  113.0 0.1 collective-permute-start.4
  113.1 1.2 collective-permute-done.4.other
  114.4 0.7 last_rows.1
  115.1 14.1 %all_to_all.71 = f32[64,1,128]{2,1,0:T(1,128)S(1)} all-to-all(f32[64,1,128]{2,1,0:T(1,128)S(1)} %bitcast.86), channel_id=1, replica_groups=mesh['rows'=64,'feat'=2] {'rows'}, dimensions={0} | all-to-all | bytes 65536 | tf_op jit(solution)/shard_map/all_to_all | solution.py:471
  129.2 0.0 copy-start.6
  129.2 0.0 copy-start.7
  129.2 2.1 %combine.1 = (f32[4096,128]{1,0:T(8,128)}, f32[1,1]{1,0:T(1,128)}) custom-call(bf16[64,72,128]{2,1,0:T(8,128)(2,1)S(1)} %all_to_all.68.recv.recv0, bf16[64,72,128]{2,1,0:T(8,128)(2,1)S(1)} %all_to_all.70.recv.recv1, f32[4096,128]{1,0:T(8,128)S(1)} %copy-done.1, f32[64,128]{1,0:T(8,128)S(1)} %bitcast.85, f32[8,128]{1,0:T(8,128)S(1)} %get-tuple-element.181.scal.beta0, ...), custom_call_target="tpu_custom_call" | custom-call | tf_op jit(solution)/shard_map/combine/pallas_call | solution.py:553
  131.3 0.0 copy-done.6
  131.3 0.0 copy-done.7
  131.3 0.8 while.36
Async XLA Ops:
  0.6 32.5 %copy-start.1 = (f32[4096,128]{1,0:T(8,128)S(1)}, f32[4096,128]{1,0:T(8,128)}, u32[]{:S(2)}) copy-start(f32[4096,128]{1,0:T(8,128)} %scale.1) | copy-start | bytes 6291460
  56.8 5.9 %copy-start.4 = (f32[128,128]{1,0:T(8,128)S(1)}, f32[128,128]{1,0:T(8,128)}, u32[]{:S(2)}) copy-start(f32[128,128]{1,0:T(8,128)} %weight.3) | copy-start | bytes 196612
  56.8 5.9 %copy-start.5 = (s32[128,128]{1,0:T(8,128)S(1)}, s32[128,128]{1,0:T(8,128)}, u32[]{:S(2)}) copy-start(s32[128,128]{1,0:T(8,128)} %labels.1) | copy-start | bytes 196612
  61.3 1.3 %collective-permute-start.3 = (f32[136,128]{1,0:T(8,128)S(1)}, f32[136,128]{1,0:T(8,128)S(1)}, u32[]{:S(2)}, u32[]{:S(2)}) collective-permute-start(f32[136,128]{1,0:T(8,128)S(1)} %forward.2.mine), channel_id=1, source_target_pairs={{0,1},{1,0},{2,3},{3,2},{4,5},{5,4},{6,7},{7,6},{8,9},{9,8},{10,11... | collective-permute-start | bytes 208904 | tf_op jit(solution)/shard_map/ppermute | solution.py:474
  113.0 1.3 %collective-permute-start.4 = (f32[136,128]{1,0:T(8,128)S(1)}, f32[136,128]{1,0:T(8,128)S(1)}, u32[]{:S(2)}, u32[]{:S(2)}) collective-permute-start(f32[136,128]{1,0:T(8,128)S(1)} %forward.3.mine), channel_id=1, source_target_pairs={{0,1},{1,0},{2,3},{3,2},{4,5},{5,4},{6,7},{7,6},{8,9},{9,8},{10,11... | collective-permute-start | bytes 208904 | tf_op jit(solution)/shard_map/ppermute | solution.py:474
  129.2 2.1 %copy-start.6 = (s32[128,1]{0,1:T(1,128)S(1)}, s32[128,1]{0,1:T(1,128)}, u32[]{:S(2)}) copy-start(s32[128,1]{0,1:T(1,128)} %param.12) | copy-start | bytes 1540
  129.2 2.2 %copy-start.7 = (s32[128,4]{0,1:T(4,128)S(1)}, s32[128,4]{0,1:T(4,128)}, u32[]{:S(2)}) copy-start(s32[128,4]{0,1:T(4,128)} %param.11) | copy-start | bytes 6148
